TPU v7x, 256 devices: a whole 4x4x8 slice. The times are simulated.
256 devices in a mesh: rows: 32 (over z, x), tensor: 8 (over y, core).
Axes of the slice: x: 4, y: 4, z: 8, core: 2. Of those that a mesh axis runs over, the one named last changes fastest.
Arguments:
- context: bfloat16 [2, 5120, 4096], P(None, 'rows', 'tensor'), may hold values from -6 to 6
- o_weight: bfloat16 [4096, 8192], P('tensor'), may hold values from -0.125 to 0.125
- residual: bfloat16 [2, 5120, 8192], P(None, 'rows', 'tensor'), may hold values from -6 to 6
- counts: int32 [2, 1024], P(None, 'rows'), may hold values from 0 to 5
- slots: int32 [2, 5120], P(None, 'rows'), may hold values from 0 to 5119, as said below
- fc_weight: bfloat16 [2048, 8192], P('rows', 'tensor'), may hold values from -0.0625 to 0.0625
- gain: float32 [2048], replicated, may hold values from 0.1 to 1.9
- goal: bfloat16 [2, 5120, 2048], P(None, 'rows'), may hold values from -6 to 6
Outputs:
- verified: float32 [2, 5120, 8192], P(None, 'rows', 'tensor')
- draft_out: float32 [2, 5120, 2048], P(None, 'rows', 'tensor')
- fc_grad: float32 [2048, 8192], P('rows', 'tensor')
Inputs may be any that keep to these rules, and one draw needn't show every extreme that they name: In each step the slots of all rows are a permutation of 0 to 5119. Slot i belongs to trainer device i // 160; the rows of device p take, on every trainer device, exactly the 5 slots from p * 5 to (p + 1) * 5 - 1 of that device's block.
All inputs are finite; a program needn't handle non-finite values.
Results may differ from a plain program's by a relative error of at most 0.014.
Values may be sent and summed in bfloat16 or wider, within the bound.
No kernel may reach another device: no remote copies, remote signals or barrier semaphores. Data moves between devices by JAX's collectives and lax.ppermute only.
A program may use at most 64 MiB of HBM per device.

v0:
```python
import math

import jax
import jax.numpy as jnp
from jax import lax
from jax.sharding import PartitionSpec as P

K = 5
STEPS = 2


epsilon = 1e-06


def draft_norm(summed, gain, goal, weight):
    mean_square = jnp.mean(summed * summed, axis=-1, keepdims=True)
    inverse = lax.rsqrt(mean_square + epsilon)
    normed = summed * inverse * gain
    error = normed - goal.astype(jnp.float32)
    pulled = gain * (weight * error)
    spread = jnp.mean(summed * pulled, axis=-1, keepdims=True)
    back = inverse * (pulled - summed * (inverse * inverse) * spread)
    return (normed, back.astype(jnp.bfloat16))


def grad_term(back_rows, input_rows):
    return lax.dot_general(
        back_rows, input_rows, (((0,), (0,)), ((), ())), preferred_element_type=jnp.float32
    )


def local(context, o_weight, residual, counts, slots, fc_weight, gain, goal):
    row_count = lax.axis_size("rows")
    rows_dev = context.shape[1]
    width = residual.shape[2]
    per_peer = rows_dev // row_count
    source = lax.axis_index("rows")
    weight = 1.0 / math.sqrt(STEPS * rows_dev * row_count)
    offsets = jnp.arange(rows_dev, dtype=jnp.int32) % K
    verified = []
    arrivals = []
    for step in range(STEPS):
        head_terms = jnp.dot(context[step], o_weight, preferred_element_type=jnp.float32)
        projected = lax.psum_scatter(
            head_terms.astype(jnp.bfloat16), "tensor", scatter_dimension=1, tiled=True
        ).astype(jnp.float32)
        full_state = residual[step].astype(jnp.float32) + projected
        verified.append(full_state)
        hidden = full_state.astype(jnp.bfloat16)
        accepted = offsets < jnp.repeat(counts[step], K)
        masked = jnp.where(accepted[:, None], hidden, jnp.zeros_like(hidden))
        slot_ids = slots[step]
        position = slot_ids // rows_dev * per_peer + slot_ids % rows_dev - source * per_peer
        outgoing = jnp.zeros_like(masked).at[position].set(masked)
        arrived = lax.all_to_all(
            outgoing.reshape(row_count, per_peer, width),
            "rows",
            split_axis=0,
            concat_axis=0,
            tiled=True,
        )
        arrivals.append(arrived.reshape(rows_dev, width))
    trained = jnp.concatenate(arrivals, 0)
    draft_terms = lax.dot_general(
        trained,
        lax.all_gather(fc_weight, "rows", axis=0, tiled=True),
        (((1,), (1,)), ((), ())),
        preferred_element_type=jnp.float32,
    )
    goal_rows = goal.reshape(STEPS * rows_dev, goal.shape[2])
    summed = lax.psum(draft_terms, "tensor")
    normed, back = draft_norm(summed, gain, goal_rows, weight)
    feature = normed.shape[1] // lax.axis_size("tensor")
    own_normed = lax.dynamic_slice_in_dim(normed, lax.axis_index("tensor") * feature, feature, 1)
    grad = lax.psum_scatter(grad_term(back, trained), "rows", scatter_dimension=0, tiled=True)
    draft_out = own_normed.reshape(STEPS, rows_dev, own_normed.shape[1])
    return (jnp.stack(verified), draft_out, grad)


def solution(mesh):
    placed = (
        P(None, "rows", "tensor"),
        P("tensor", None),
        P(None, "rows", "tensor"),
        P(None, "rows"),
        P(None, "rows"),
        P("rows", "tensor"),
        P(),
        P(None, "rows", None),
    )
    return jax.shard_map(
        local,
        mesh=mesh,
        in_specs=placed,
        out_specs=(P(None, "rows", "tensor"), P(None, "rows", "tensor"), P("rows", "tensor")),
        check_vma=False,
    )
```

profile of v0, /device:TPU:16, one launch (start us, length us, event | category | flops | bytes accessed | tf_op | source)
XLA Modules:
  0.0 445.8 jit_solution(13486977306910474603)
XLA Ops:
  8.0 6.6 %convolution_convert_fusion = bf16[160,8192]{1,0:T(8,128)(2,1)} fusion(bf16[512,8192]{1,0:T(8,128)(2,1)} %param.9, bf16[2,160,512]{2,1,0:T(8,128)(2,1)} %param.8), kind=kOutput, calls=%fused_computation.2 | convolution fusion | flops 1343488000 | bytes 11173888 | tf_op jit(solution)/shard_map/dot_general | solution.py:43
  14.7 0.9 copy-done.5
  15.6 6.5 %convolution_convert_fusion.1 = bf16[160,8192]{1,0:T(8,128)(2,1)} fusion(bf16[512,8192]{1,0:T(8,128)(2,1)} %param.9, bf16[2,160,512]{2,1,0:T(8,128)(2,1)S(1)} %copy-done.5), kind=kOutput, calls=%fused_computation.3 | convolution fusion | flops 1343488000 | bytes 11173888 | tf_op jit(solution)/shard_map/dot_general | solution.py:43
  22.1 0.5 all-gather.2.cloned.1.call-update
  22.7 0.1 broadcast_in_dim.29
  22.8 0.1 reshape.235
  23.0 27.1 %reduce-scatter.6.cloned.1.call-done = bf16[160,1024]{1,0:T(8,128)(2,1)} async-done(((bf16[160,8192]{1,0:T(8,128)(2,1)}), bf16[160,1024]{1,0:T(8,128)(2,1)}) %reduce-scatter.6.cloned.1.call-update) | async-done | bytes 327696 | tf_op jit(solution)/shard_map/reduce_scatter | solution.py:44
  50.1 1.9 scatter_custom_fusion.1
  52.0 0.9 reshape.236
  52.9 9.9 %all-to-all-start.1 = ((bf16[32,5,1024]{2,1,0:T(8,128)(2,1)}), bf16[32,5,1024]{2,1,0:T(8,128)(2,1)S(1)}, u32[]{:S(2)}, u32[]{:S(2)}) async-start(bf16[32,5,1024]{2,1,0:T(8,128)(2,1)} %reshape.236), calls=%async_computation.3 | async-start | bytes 1048576 | tf_op jit(solution)/shard_map/all_to_all | solution.py:55
  62.8 0.1 reshape.232
  63.0 26.5 %reduce-scatter.4.cloned.1.call-done = bf16[160,1024]{1,0:T(8,128)(2,1)} async-done(((bf16[160,8192]{1,0:T(8,128)(2,1)}), bf16[160,1024]{1,0:T(8,128)(2,1)}) %reduce-scatter.4.cloned.1.call-update) | async-done | bytes 327696 | tf_op jit(solution)/shard_map/reduce_scatter | solution.py:44
  89.5 1.9 scatter_custom_fusion
  91.4 0.9 reshape.233
  92.3 9.8 %all-to-all-start = ((bf16[32,5,1024]{2,1,0:T(8,128)(2,1)}), bf16[32,5,1024]{2,1,0:T(8,128)(2,1)S(1)}, u32[]{:S(2)}, u32[]{:S(2)}) async-start(bf16[32,5,1024]{2,1,0:T(8,128)(2,1)} %reshape.233), calls=%async_computation.2 | async-start | bytes 1048576 | tf_op jit(solution)/shard_map/all_to_all | solution.py:55
  102.1 0.1 reshape.237
  102.3 18.6 %all-to-all-done = bf16[32,5,1024]{2,1,0:T(8,128)(2,1)S(1)} async-done(((bf16[32,5,1024]{2,1,0:T(8,128)(2,1)}), bf16[32,5,1024]{2,1,0:T(8,128)(2,1)S(1)}, u32[]{:S(2)}, u32[]{:S(2)}) %all-to-all-start) | async-done | bytes 327712 | tf_op jit(solution)/shard_map/all_to_all | solution.py:55
  120.9 0.1 reshape.234
  121.1 5.3 %fusion.32 = f32[320,2048]{1,0:T(8,128)} fusion(bf16[320,1024]{1,0:T(8,128)(2,1)S(1)} %constant_dynamic-update-slice_fusion, bf16[2048,1024]{1,0:T(8,128)(2,1)} %all-gather.2.cloned.1.call-done), kind=kOutput, calls=%fused_computation.57 | convolution fusion | flops 1342177280 | bytes 7471104 | tf_op jit(solution)/shard_map/dot_general | solution.py:64
  126.5 0.2 reduce-scatter.8.cloned.1.call-start
  126.7 0.4 copy-done.6
  127.1 65.7 %all-reduce.2.cloned.1.call-done = f32[320,2048]{1,0:T(8,128)} async-done(((f32[320,2048]{1,0:T(8,128)}), f32[320,2048]{1,0:T(8,128)}) %all-reduce.2.cloned.1.call-update) | async-done | bytes 2621456 | tf_op jit(solution)/shard_map/psum | solution.py:71
  192.8 2.2 multiply_reduce_fusion.1
  195.0 0.4 copy-done
  195.4 2.3 multiply_reduce_fusion
  197.7 6.1 %fusion.1 = f32[2048,1024]{1,0:T(8,128)} fusion(bf16[320,1024]{1,0:T(8,128)(2,1)S(1)} %constant_dynamic-update-slice_fusion, f32[320,2048]{1,0:T(8,128)S(1)} %copy-done, bf16[320,2048]{1,0:T(8,128)(2,1)S(1)} %bitcast.79, f32[320]{0:T(512)S(1)} %broadcast_multiply_fusion.1, f32[320]{0:T(512)S(1)} %get-tuple-element.7, f32[2048]{0:T(1024)S(1)} %broadcast_multiply_fusion, ...), kind=kOutput, calls=%fused_computation.10 | convolution fusion | flops 1348730880 | bytes 12996352 | tf_op jit(solution)/shard_map/dot_general | solution.py:27
  203.8 0.9 copy-done.3
  204.8 0.1 copy-done.4
  204.9 0.2 fusion.8
  205.1 1.1 pad_maximum_fusion
  206.2 1.7 constant_dynamic-slice_fusion
  208.0 230.7 %reduce-scatter.8.cloned.1.call-done = f32[64,1024]{1,0:T(8,128)} async-done(((f32[2048,1024]{1,0:T(8,128)}), f32[64,1024]{1,0:T(8,128)}) %reduce-scatter.8.cloned.1.call-update) | async-done | bytes 262160 | tf_op jit(solution)/shard_map/reduce_scatter | solution.py:75
  (33 shorter events, 0.5 us)
Async XLA Ops:
  8.0 42.1 %reduce-scatter.6.cloned.1.call-start = ((), (), s32[]{:S(2)}) async-start(), calls=%async_computation.6 | async-start | bytes 2949120 | tf_op jit(solution)/shard_map/reduce_scatter | solution.py:44
  14.6 1.0 copy-start.5
  14.6 74.9 %reduce-scatter.4.cloned.1.call-start = ((), (), s32[]{:S(2)}) async-start(), calls=%async_computation.5 | async-start | bytes 2949120 | tf_op jit(solution)/shard_map/reduce_scatter | solution.py:44
  22.1 0.7 copy-start.8
  22.1 0.9 copy-start.7
  22.1 28.0 %copy-start.2 = (bf16[2,160,1024]{2,1,0:T(8,128)(2,1)S(1)}, bf16[2,160,1024]{2,1,0:T(8,128)(2,1)}, u32[]{:S(2)}) copy-start(bf16[2,160,1024]{2,1,0:T(8,128)(2,1)} %param.10) | copy-start | bytes 1966084
  22.1 99.0 %all-gather.2.cloned.1.call-start = ((), (), s32[]{:S(2)}) async-start(), calls=%async_computation.7 | async-start | bytes 4325376 | tf_op jit(solution)/shard_map/all_gather | solution.py:66
  52.9 39.4 %all-to-all-start.1 = ((bf16[32,5,1024]{2,1,0:T(8,128)(2,1)}), bf16[32,5,1024]{2,1,0:T(8,128)(2,1)S(1)}, u32[]{:S(2)}, u32[]{:S(2)}) async-start(bf16[32,5,1024]{2,1,0:T(8,128)(2,1)} %reshape.236), calls=%async_computation.3 | async-start | bytes 1048576 | tf_op jit(solution)/shard_map/all_to_all | solution.py:55
  92.3 28.6 %all-to-all-start = ((bf16[32,5,1024]{2,1,0:T(8,128)(2,1)}), bf16[32,5,1024]{2,1,0:T(8,128)(2,1)S(1)}, u32[]{:S(2)}, u32[]{:S(2)}) async-start(bf16[32,5,1024]{2,1,0:T(8,128)(2,1)} %reshape.233), calls=%async_computation.2 | async-start | bytes 1048576 | tf_op jit(solution)/shard_map/all_to_all | solution.py:55
  102.1 90.8 %all-reduce.2.cloned.1.call-start = ((), (), s32[]{:S(2)}) async-start(), calls=%async_computation.8 | async-start | bytes 5242880 | tf_op jit(solution)/shard_map/psum | solution.py:71
  126.4 0.7 copy-start.6
  126.4 68.6 %copy-start.1 = (bf16[2,160,2048]{2,1,0:T(8,128)(2,1)S(1)}, bf16[2,160,2048]{2,1,0:T(8,128)(2,1)}, u32[]{:S(2)}) copy-start(bf16[2,160,2048]{2,1,0:T(8,128)(2,1)} %param.15) | copy-start | bytes 3932164
  126.5 312.2 %reduce-scatter.8.cloned.1.call-start = ((), (), s32[]{:S(2)}) async-start(), calls=%async_computation.9 | async-start | bytes 8650752 | tf_op jit(solution)/shard_map/reduce_scatter | solution.py:75
  192.8 2.5 copy-start
  203.8 1.0 copy-start.3
  203.8 1.1 copy-start.4
Sparse Core Ops, SparseCore 0:
  14.8 35.2 reduce-scatter.5
  52.7 36.8 reduce-scatter.3
  126.6 66.2 all-reduce.1
Sparse Core Ops, SparseCore 1:
  25.2 88.3 all-gather.1
  203.9 234.7 reduce-scatter.7
where the time goes:
time: 446 us
  waiting for transfers between devices  369 us (83%)
  matrix products  24.5 us (5%)
  starting transfers between devices  20 us (4%)
  between operations  15.3 us (3%)
  other arithmetic  9.6 us (2%)
  local copies, waits for them, and re-layouts  7.06 us (2%)
    reduce_scatter x1, waiting for transfers between devices, local(): lax.psum_scatter(grad_term(back, trained), 'rows', scatter_dimension=0, t...  231 us
    psum x1, waiting for transfers between devices, local(): summed = lax.psum(draft_terms, 'tensor')  65.7 us
    reduce_scatter x2, waiting for transfers between devices, local(): lax.psum_scatter(head_terms.astype(jnp.bfloat16), 'tensor', scatter_dimen...  53.7 us
    all_to_all x2, starting transfers between devices, local(): lax.all_to_all(outgoing.reshape(row_count, per_peer, width), 'rows', spli...  19.6 us
    all_to_all x2, waiting for transfers between devices, local(): lax.all_to_all(outgoing.reshape(row_count, per_peer, width), 'rows', spli...  18.6 us
    dot_general x2, matrix products, local(): jnp.dot(context[step], o_weight, preferred_element_type=jnp.float32)  13 us
  transfers between devices with their start and end apart: 7, of which 5 were waited for; matrix products, arithmetic and copies ran while one was open for 4% of the time, Pallas kernels for 0%

commit v1 on v0

v1 whole, which is shorter than its diff:
```python
import functools
import math

import jax
import jax.numpy as jnp
from jax import lax
from jax.experimental import pallas as pl
from jax.experimental.pallas import tpu as pltpu
from jax.sharding import Mesh, PartitionSpec as P


K = 5
STEPS = 2
NZ, NX, NY, NC = 8, 4, 4, 2
EPSILON = 1e-06
BF16 = jnp.bfloat16
F32 = jnp.float32
VMEM = pl.BlockSpec(memory_space=pltpu.VMEM)
SMEM = pl.BlockSpec(memory_space=pltpu.SMEM)


def shift(value, axis, size, by):
    return lax.ppermute(value, axis, [(i, (i + by) % size) for i in range(size)])


def swap(value):
    return shift(value, "c", NC, 1)


def exchange(value, axis):
    return lax.all_to_all(value, axis, 0, 0, tiled=True)


def take(value, index, axis=0):
    return lax.dynamic_index_in_dim(value, index, axis, False)


def project_kernel(blocks, parts, adds, place_ref, ctx_ref, weight_ref, *refs):
    added, outs, (held, sems) = refs[:adds], list(refs[adds:-2]), refs[-2:]
    width = held.shape[2]
    count = len(blocks)
    copies = []
    for i, (d, other) in enumerate(blocks):
        core = 1 - place_ref[1] if other else place_ref[1]
        block = lax.rem(place_ref[0] + d, NY) * NC + core
        span = pl.ds(pl.multiple_of(block * width, width), width)
        copies.append(pltpu.make_async_copy(weight_ref.at[:, span], held.at[i], sems.at[i]))
        copies[-1].start()
    for i in range(count):
        copies[i].wait()
        product = jnp.dot(ctx_ref[...], held[i], preferred_element_type=F32)
        if adds:
            product = product + added[i][...].astype(F32)
        step = width // parts[i]
        for h in range(parts[i]):
            out = outs.pop(0)
            out[...] = product[:, h * step:(h + 1) * step].astype(out.dtype)


def project(place, blocks, ctx, weight, width, added, types):
    count, (rows, depth) = len(blocks), ctx.shape
    parts = [len(t) for t in types]
    return pl.pallas_call(
        functools.partial(project_kernel, blocks, parts, len(added)),
        in_specs=[SMEM, VMEM, pl.BlockSpec(memory_space=pl.ANY)] + [VMEM] * len(added),
        out_specs=[VMEM] * sum(parts),
        out_shape=[jax.ShapeDtypeStruct((rows, width // len(ts)), t) for ts in types for t in ts],
        scratch_shapes=[
            pltpu.VMEM((count, depth, width), weight.dtype),
            pltpu.SemaphoreType.DMA((count,)),
        ],
        cost_estimate=pl.CostEstimate(
            flops=2 * count * rows * depth * width,
            bytes_accessed=2 * count * (depth + rows) * width,
            transcendentals=0,
        ),
        name="project",
    )(place, ctx, weight, *added)


def merge_kernel(near_up, far_up, early_up, early_down, near_down, far_down, up, down):
    half = near_up.shape[1]
    up[:, :half] = (near_up[...] + far_up[...].astype(F32)).astype(up.dtype)
    up[:, half:] = early_up[...]
    down[:, :half] = early_down[...]
    down[:, half:] = (near_down[...] + far_down[...].astype(F32)).astype(down.dtype)


def merge(*parts):
    rows, half = parts[0].shape
    return pl.pallas_call(
        merge_kernel,
        in_specs=[VMEM] * len(parts),
        out_specs=[VMEM] * 2,
        out_shape=[jax.ShapeDtypeStruct((rows, 2 * half), BF16)] * 2,
        cost_estimate=pl.CostEstimate(flops=rows * half, bytes_accessed=18 * rows * half, transcendentals=0),
        name="merge",
    )(*parts)


def local(context, o_weight, residual, counts, slots, fc_weight, gain, goal):
    z, x, y, c = (lax.axis_index(name) for name in ("z", "x", "y", "c"))
    rows = context.shape[1]
    width = residual.shape[2]
    per_peer = rows // (NZ * NX)
    feats = fc_weight.shape[0]
    some = NZ * feats
    draft_width = gain.shape[0]
    weight = 1.0 / math.sqrt(STEPS * rows * NZ * NX)

    ctx = context.reshape(STEPS * rows, context.shape[2])
    half = width // 2
    place = jnp.stack([y, c]).astype(jnp.int32)
    blocks = ((2, True), (2, False), (1, True), (3, True), (0, True))
    first, *far_own, one, three, zero = project(
        place, blocks, ctx, o_weight, width, [], [[BF16], [F32, F32], [BF16], [BF16], [BF16]]
    )
    first, one, three, zero = swap(first), swap(one), swap(three), swap(zero)
    far = [(far_own[h] + first[:, h * half:(h + 1) * half].astype(F32)).astype(BF16) for h in range(2)]
    near = project(
        place, ((1, False), (3, False)), ctx, o_weight, width, [one, three], [[F32, BF16], [BF16, F32]]
    )
    own = project(place, ((0, False),), ctx, o_weight, width, [zero], [[F32]])[0]

    far_up = shift(far[0], "y", NY, 1)
    far_down = shift(far[1], "y", NY, -1)
    up, down = merge(near[0], far_up, near[1], near[2], near[3], far_down)
    up, down, fc_weight, goal = lax.optimization_barrier((up, down, fc_weight, goal))
    up = shift(up, "y", NY, 1)
    down = shift(down, "y", NY, -1)

    slot = per_peer + -per_peer % 8
    chosen = jnp.arange(NZ * slot, dtype=jnp.int32)
    chosen = jnp.where(chosen % slot < per_peer, (chosen // slot * NX + y) * per_peer + chosen % slot, -1)
    chosen = (chosen[:, None] == jnp.arange(rows, dtype=jnp.int32)).astype(BF16)
    target = jnp.dot(chosen, take(goal, c), preferred_element_type=F32).astype(BF16)
    cuts = [target[:, i:i + width].reshape(NZ, slot, width) for i in range(0, draft_width, width)]
    load = jnp.concatenate([jnp.broadcast_to(fc_weight, (NZ, feats, width)), *cuts], 1)
    load = exchange(load, "z")
    fc_all = load[:, :feats].reshape(some, width)
    cuts = [load[:, feats + i * slot:feats + (i + 1) * slot] for i in range(draft_width // width)]
    target = jnp.concatenate(cuts, 2).reshape(NZ * slot, NZ, NX, feats).transpose(2, 0, 1, 3)
    target = exchange(target.reshape(NX, NZ * slot, some), "x").reshape(-1, some)
    packed = jnp.arange(rows, dtype=jnp.int32)
    peer = packed // per_peer
    packed = (peer % NX * NZ + peer // NX) * slot + packed % per_peer
    packed = packed[:, None] == jnp.arange(target.shape[0], dtype=jnp.int32)
    target = jnp.dot(packed.astype(BF16), target, preferred_element_type=F32)

    source = z * NX + x
    position = slots // rows * per_peer + slots % rows - source * per_peer
    accepted = jnp.arange(rows, dtype=jnp.int32) % K < jnp.repeat(counts, K, axis=1)
    position = jnp.where(accepted, position, -1)
    pick = (position[:, None, :] == jnp.arange(rows, dtype=jnp.int32)[None, :, None]).astype(BF16)

    total = own + up.astype(F32) + down.astype(F32)
    verified = residual.astype(F32) + total.reshape(STEPS, rows, width)
    own = lax.dot_general(
        pick, verified.astype(BF16), (((2,), (1,)), ((0,), (0,))), preferred_element_type=F32
    ).astype(BF16)

    right = shift(own, "x", NX, -1)
    left = shift(own, "x", NX, 1)
    opposite = jnp.concatenate([shift(right[:1], "x", NX, -1), shift(left[1:], "x", NX, 1)], 0)
    trained = jnp.stack([own, right, opposite, left])
    trained, target = lax.optimization_barrier((trained.reshape(NX * STEPS * rows, width), target))

    partial = lax.dot_general(
        trained, fc_all, (((1,), (1,)), ((), ())), preferred_element_type=F32
    ).astype(BF16).reshape(NX, STEPS, rows, some)
    given = swap(take(partial, 1 - c, 1))
    kept = take(partial, c, 1)

    def term(i):
        m = (i - x + NX) % NX
        return (take(kept, m).astype(F32) + take(given, m).astype(F32)).astype(BF16)

    summed = jnp.stack([term(i) for i in range(NY)])
    summed = exchange(summed, "y").astype(F32).sum(0)

    scale = take(gain.reshape(NZ, NX, feats), x, 1).reshape(1, some)
    scaled = summed * scale
    sums = jnp.stack(
        [jnp.sum(summed * summed, -1), jnp.sum(scaled * scaled, -1), jnp.sum(scaled * target, -1)]
    )
    sums = exchange(jnp.broadcast_to(sums, (NX, *sums.shape)), "x").sum(0)
    mean_square, gained, aimed = sums[0] / draft_width, sums[1] / draft_width, sums[2] / draft_width
    inverse = lax.rsqrt(mean_square + EPSILON)[:, None]
    spread = weight * (inverse * gained[:, None] - aimed[:, None])
    normed = summed * inverse * scale
    pulled = scale * (weight * (normed - target))
    back = (inverse * (pulled - summed * (inverse * inverse) * spread)).astype(BF16)

    normed = normed.astype(BF16)
    pair = NC * feats
    load = jnp.stack([jnp.concatenate([back, normed[:, i * pair:(i + 1) * pair]], 1) for i in range(NY)])
    load = exchange(load, "y")
    both = jnp.stack([load, swap(load)])
    both = jnp.stack([take(both, (s + c) % NC) for s in range(NC)], 1)
    lined = jnp.stack([take(both, (m + x) % NX) for m in range(NX)])
    terms = lax.dot_general(
        lined[:, :, :, :some].reshape(NX * STEPS * rows, some),
        trained,
        (((0,), (0,)), ((), ())),
        preferred_element_type=F32,
    )

    def block(m):
        return lax.dynamic_slice_in_dim(terms, (z + m) % NZ * feats, feats, 0)

    grad = block(0)
    arrived = {m: shift(block(m).astype(BF16), "z", NZ, m) for m in (4, 3, 5, 2, 6, 1)}
    arrived[7] = shift(block(7).astype(BF16), "z", NZ, 7)
    for m in (1, 7, 2, 6, 3, 5, 4):
        grad = grad + arrived[m].astype(F32)

    out = lax.dynamic_slice_in_dim(both[:, :, :, some:], c * feats, feats, 3)
    out = out.reshape(NX * STEPS, NZ * NX, per_peer, feats).transpose(1, 0, 2, 3)
    out = exchange(out.reshape(NZ * NX, NX * STEPS * per_peer, feats), ("z", "x"))
    out = out.reshape(NZ, NX, NX, STEPS, per_peer, feats).transpose(3, 0, 2, 4, 1, 5)
    draft_out = out.reshape(STEPS, rows, NX * feats).astype(F32)
    return verified, draft_out, grad


def solution(mesh):
    grid = Mesh(mesh.devices.reshape(NZ, NX, NY, NC), ("z", "x", "y", "c"))
    r, t = ("z", "x"), ("y", "c")
    placed = (
        P(None, r, t),
        P(t, None),
        P(None, r, t),
        P(None, r),
        P(None, r),
        P(r, t),
        P(),
        P(None, r, None),
    )

    return jax.shard_map(
        local,
        mesh=grid,
        in_specs=placed,
        out_specs=(P(None, r, t), P(None, r, t), P(r, t)),
        check_vma=False,
    )
```

time: 446 us -> 200 us (0.45)
  waiting for transfers between devices: 369 us -> 55.2 us
  starting transfers between devices: 20 us -> 62.4 us
  matrix products: 24.5 us -> 5.96 us
  Pallas kernels: 0 us -> 17.6 us
  between operations: 15.3 us -> 1.16 us
  blocking collectives: 0 us -> 14.1 us
  local copies, waits for them, and re-layouts: 7.06 us -> 21.1 us
  other arithmetic: 9.6 us -> 20 us
    reduce_scatter x3 -> x0, waiting for transfers between devices: 284 us -> none  [the longest x1 231 us: local(): lax.psum_scatter(grad_term(back, trained), 'rows', scatter_dimension=0, t...]
    psum x1 -> x0, waiting for transfers between devices: 65.7 us -> none  [local(): summed = lax.psum(draft_terms, 'tensor')]
    ppermute x0 -> x21, starting transfers between devices: none -> 33.7 us  [shift(): lax.ppermute(value, axis, [(i, (i + by) % size) for i in range(size)])]
    ppermute x0 -> x21, waiting for transfers between devices: none -> 30.5 us  [shift(): lax.ppermute(value, axis, [(i, (i + by) % size) for i in range(size)])]
    dot_general x4 -> x5, matrix products: 24.5 us -> 5.96 us  [the longest x1 3.58 us: local(): lax.dot_general(trained, fc_all, (((1,), (1,)), ((), ())), preferred_elem...]
    pallas_call x0 -> x4, Pallas kernels: none -> 17.6 us  [the longest x3 14.8 us: project(): pl.pallas_call(functools.partial(project_kernel, blocks, parts, len(added...]
    all_to_all x0 -> x1, blocking collectives: none -> 14.1 us  [exchange(): return lax.all_to_all(value, axis, 0, 0, tiled=True)]
    all_to_all x2 -> x5, starting transfers between devices: 19.6 us -> 28.7 us  [exchange(): return lax.all_to_all(value, axis, 0, 0, tiled=True)]
  transfers between devices with their start and end apart: 7 -> 26, of which waited for: 5 -> 13; matrix products, arithmetic and copies ran while one was open for 4% -> 9% of each run, Pallas kernels for 0% -> 6%
where the time goes in v1:
time: 200 us; the launch traced here: 197 us
  starting transfers between devices  62.4 us (31%)
  waiting for transfers between devices  55.2 us (28%)
  local copies, waits for them, and re-layouts  21.1 us (11%)
  other arithmetic  20 us (10%)
  Pallas kernels  17.6 us (9%)
  blocking collectives  14.1 us (7%)
  matrix products  5.96 us (3%)
    ppermute x21, starting transfers between devices, shift(): lax.ppermute(value, axis, [(i, (i + by) % size) for i in range(size)])  33.7 us
    ppermute x21, waiting for transfers between devices, shift(): lax.ppermute(value, axis, [(i, (i + by) % size) for i in range(size)])  30.5 us
    all_to_all x5, starting transfers between devices, exchange(): return lax.all_to_all(value, axis, 0, 0, tiled=True)  28.7 us
    all_to_all x5, waiting for transfers between devices, exchange(): return lax.all_to_all(value, axis, 0, 0, tiled=True)  24.6 us
    pallas_call x3, Pallas kernels, project(): pl.pallas_call(functools.partial(project_kernel, blocks, parts, len(added...  14.8 us
    all_to_all x1, blocking collectives, exchange(): return lax.all_to_all(value, axis, 0, 0, tiled=True)  14.1 us
    unnamed x37, local copies, waits for them, and re-layouts  8.54 us
    another operation x2, other arithmetic, local(): trained = jnp.stack([own, right, opposite, left])  5.26 us
  transfers between devices with their start and end apart: 26, of which 13 were waited for; matrix products, arithmetic and copies ran while one was open for 9% of the time, Pallas kernels for 6%

profile of v1, /device:TPU:16, one launch (start us, length us, event | category | flops | bytes accessed | tf_op | source)
XLA Modules:
  0.0 197.5 jit_solution(13451815717294367019)
XLA Ops:
  1.2 6.2 %project.3 = (bf16[320,1024]{1,0:T(8,128)(2,1)}, f32[320,512]{1,0:T(8,128)}, f32[320,512]{1,0:T(8,128)}, bf16[320,1024]{1,0:T(8,128)(2,1)}, bf16[320,1024]{1,0:T(8,128)(2,1)}, /*index=5*/bf16[320,1024]{1,0:T(8,128)(2,1)}) custom-call(s32[2]{0:T(128)} %pad_add_fusion.place_ref, bf16[320,512]{1,0:T(8,128)(2,1)} %bitcast.77, bf16[512,8192]{1,0:T(8,128)(2,1)} %weight_ref.5), custom_call_target="tpu_custom_call" | custom-call | flops 1677721600 | bytes 8519680 | tf_op jit(solution)/shard_map/project/pallas_call | solution.py:63
  9.8 2.3 %add_convert_fusion = (bf16[320,512]{1,0:T(8,128)(2,1)}, bf16[320,512]{1,0:T(8,128)(2,1)}) fusion(f32[320,512]{1,0:T(8,128)} %get-tuple-element.30, bf16[320,1024]{1,0:T(8,128)(2,1)S(1)} %collective-permute-done.3, f32[320,512]{1,0:T(8,128)} %get-tuple-element.25), kind=kLoop, calls=%fused_computation.36 | loop fusion | flops 983040 | bytes 2621440 | tf_op jit(solution)/shard_map/convert_element_type | solution.py:119
  15.9 4.5 %project.5 = (f32[320,512]{1,0:T(8,128)}, bf16[320,512]{1,0:T(8,128)(2,1)}, bf16[320,512]{1,0:T(8,128)(2,1)}, f32[320,512]{1,0:T(8,128)}) custom-call(s32[2]{0:T(128)} %pad_add_fusion.place_ref, bf16[320,512]{1,0:T(8,128)(2,1)} %bitcast.78, bf16[512,8192]{1,0:T(8,128)(2,1)} %weight_ref.5, bf16[320,1024]{1,0:T(8,128)(2,1)} %copy-done.8, ...), custom_call_target="tpu_custom_call" | custom-call | flops 671088640 | bytes 3407872 | tf_op jit(solution)/shard_map/project/pallas_call | solution.py:63
  23.4 2.8 %merge.1 = (bf16[320,1024]{1,0:T(8,128)(2,1)}, bf16[320,1024]{1,0:T(8,128)(2,1)}) custom-call(f32[320,512]{1,0:T(8,128)} %get-tuple-element.24.near_up, bf16[320,512]{1,0:T(8,128)(2,1)} %collective-permute-done.4.far_up, bf16[320,512]{1,0:T(8,128)(2,1)} %get-tuple-element.27.early_up, bf16[320,512]{1,0:T(8,128)(2,1)} %get-tuple-element.28.early_down, ...), custom_call_target="tpu_custom_call" | custom-call | flops 163840 | bytes 2949120 | tf_op jit(solution)/shard_map/merge/pallas_call | solution.py:91
  26.8 2.4 %collective-permute-start.6 = (bf16[320,1024]{1,0:T(8,128)(2,1)}, bf16[320,1024]{1,0:T(8,128)(2,1)}, u32[]{:S(2)}, u32[]{:S(2)}) collective-permute-start(bf16[320,1024]{1,0:T(8,128)(2,1)} %get-tuple-element.33), channel_id=1, source_target_pairs={{0,2},{2,4},{4,6},{6,0},{1,3},{3,5},{5,7},{7,1},{8,10},{10,12},{12... | collective-permute-start | bytes 1966088 | tf_op jit(solution)/shard_map/ppermute | solution.py:23
  30.9 7.5 %all-to-all-start = ((bf16[8,80,1024]{2,1,0:T(8,128)(2,1)}), bf16[8,80,1024]{2,1,0:T(8,128)(2,1)S(1)}, u32[]{:S(2)}, u32[]{:S(2)}) async-start(bf16[8,80,1024]{2,1,0:T(8,128)(2,1)} %pad_maximum_fusion.4), calls=%async_computation | async-start | bytes 2621440 | tf_op jit(solution)/shard_map/all_to_all | solution.py:31
  39.5 4.0 %project.4 = f32[320,1024]{1,0:T(8,128)} custom-call(s32[2]{0:T(128)} %pad_add_fusion.place_ref, bf16[320,512]{1,0:T(8,128)(2,1)} %bitcast.79, bf16[512,8192]{1,0:T(8,128)(2,1)} %weight_ref.5, bf16[320,1024]{1,0:T(8,128)(2,1)} %copy-done.11), custom_call_target="tpu_custom_call" | custom-call | flops 335544320 | bytes 1703936 | tf_op jit(solution)/shard_map/project/pallas_call | solution.py:63
  49.4 12.9 %collective-permute-done.10 = bf16[2,160,1024]{2,1,0:T(8,128)(2,1)S(1)} collective-permute-done((bf16[2,160,1024]{2,1,0:T(8,128)(2,1)S(1)}, bf16[2,160,1024]{2,1,0:T(8,128)(2,1)S(1)}, u32[]{:S(2)}, u32[]{:S(2)}) %collective-permute-start.10) | collective-permute-done | bytes 655392 | tf_op jit(solution)/shard_map/ppermute | solution.py:23
  64.2 3.1 %collective-permute-start.9 = (bf16[1,160,1024]{2,1,0:T(8,128)(2,1)}, bf16[1,160,1024]{2,1,0:T(8,128)(2,1)}, u32[]{:S(2)}, u32[]{:S(2)}) collective-permute-start(bf16[1,160,1024]{2,1,0:T(8,128)(2,1)} %slice.74), channel_id=1, source_target_pairs={{0,24},{8,0},{16,8},{24,16},{1,25},{9,1},{17,9},{25,17},{2,26},{10... | collective-permute-start | bytes 983048 | tf_op jit(solution)/shard_map/ppermute | solution.py:23
  67.3 4.4 %collective-permute-done.11 = bf16[1,160,1024]{2,1,0:T(8,128)(2,1)} collective-permute-done((bf16[1,160,1024]{2,1,0:T(8,128)(2,1)}, bf16[1,160,1024]{2,1,0:T(8,128)(2,1)}, u32[]{:S(2)}, u32[]{:S(2)}) %collective-permute-start.11) | collective-permute-done | bytes 327712 | tf_op jit(solution)/shard_map/ppermute | solution.py:23
  77.5 2.1 %reshape.249 = bf16[4,64,512]{2,1,0:T(8,128)(2,1)} reshape(bf16[4,64,8,64]{3,2,1,0:T(8,128)(2,1)} %copy.29) | data formatting | bytes 524288 | tf_op jit(solution)/shard_map/reshape | solution.py:143
  79.6 5.0 %all-to-all-start.1 = ((bf16[4,64,512]{2,1,0:T(8,128)(2,1)}), bf16[4,64,512]{2,1,0:T(8,128)(2,1)S(1)}, u32[]{:S(2)}, u32[]{:S(2)}) async-start(bf16[4,64,512]{2,1,0:T(8,128)(2,1)} %reshape.249), calls=%async_computation.1 | async-start | bytes 524288 | tf_op jit(solution)/shard_map/all_to_all | solution.py:31
  84.5 3.3 %pad_maximum_fusion = bf16[4,2,160,1024]{3,2,1,0:T(8,128)(2,1)} fusion(bf16[1,2,160,1024]{3,2,1,0:T(8,128)(2,1)} %bitcast.83, bf16[1,2,160,1024]{3,2,1,0:T(8,128)(2,1)} %maximum_bitcast_fusion, bf16[1,2,160,1024]{3,2,1,0:T(8,128)(2,1)} %bitcast.84, bf16[1,2,160,1024]{3,2,1,0:T(8,128)(2,1)S(1)} %bitcast.80), kind=kLoop, calls=%fused_computation.1 | loop fusion | flops 3932160 | bytes 5242880 | tf_op jit(solution)/shard_map/stack | solution.py:165
  88.9 2.3 %all-to-all-done.1 = bf16[4,64,512]{2,1,0:T(8,128)(2,1)S(1)} async-done(((bf16[4,64,512]{2,1,0:T(8,128)(2,1)}), bf16[4,64,512]{2,1,0:T(8,128)(2,1)S(1)}, u32[]{:S(2)}, u32[]{:S(2)}) %all-to-all-start.1) | async-done | bytes 262176 | tf_op jit(solution)/shard_map/all_to_all | solution.py:31
  91.5 3.6 %convolution_convert_fusion = bf16[1280,512]{1,0:T(8,128)(2,1)S(1)} fusion(bf16[1280,1024]{1,0:T(8,128)(2,1)} %bitcast.72, bf16[512,1024]{1,0:T(8,128)(2,1)} %bitcast.89), kind=kOutput, calls=%fused_computation | convolution fusion | flops 1342832640 | bytes 4980736 | tf_op jit(solution)/shard_map/dot_general | solution.py:168
  95.9 2.4 %collective-permute-done.12 = bf16[4,160,512]{2,1,0:T(8,128)(2,1)} collective-permute-done((bf16[4,160,512]{2,1,0:T(8,128)(2,1)}, bf16[4,160,512]{2,1,0:T(8,128)(2,1)}, u32[]{:S(2)}, u32[]{:S(2)}) %collective-permute-start.12) | collective-permute-done | bytes 655392 | tf_op jit(solution)/shard_map/ppermute | solution.py:23
  100.6 7.6 %all-to-all-start.2 = ((bf16[4,160,512]{2,1,0:T(8,128)(2,1)}), bf16[4,160,512]{2,1,0:T(8,128)(2,1)S(1)}, u32[]{:S(2)}, u32[]{:S(2)}) async-start(bf16[4,160,512]{2,1,0:T(8,128)(2,1)} %pad_maximum_fusion.6), calls=%async_computation.2 | async-start | bytes 1310720 | tf_op jit(solution)/shard_map/all_to_all | solution.py:31
  108.5 8.3 %all-to-all-done.2 = bf16[4,160,512]{2,1,0:T(8,128)(2,1)S(1)} async-done(((bf16[4,160,512]{2,1,0:T(8,128)(2,1)}), bf16[4,160,512]{2,1,0:T(8,128)(2,1)S(1)}, u32[]{:S(2)}, u32[]{:S(2)}) %all-to-all-start.2) | async-done | bytes 655392 | tf_op jit(solution)/shard_map/all_to_all | solution.py:31
  117.8 3.2 %all-to-all-start.3 = ((f32[4,1,480]{2,1,0:T(1,128)}), f32[4,1,480]{2,1,0:T(1,128)S(1)}, u32[]{:S(2)}, u32[]{:S(2)}) async-start(f32[4,1,480]{2,1,0:T(1,128)} %reshape.270), calls=%async_computation.3 | async-start | bytes 16384 | tf_op jit(solution)/shard_map/all_to_all | solution.py:31
  121.0 5.3 %all-to-all-done.3 = f32[4,1,480]{2,1,0:T(1,128)S(1)} async-done(((f32[4,1,480]{2,1,0:T(1,128)}), f32[4,1,480]{2,1,0:T(1,128)S(1)}, u32[]{:S(2)}, u32[]{:S(2)}) %all-to-all-start.3) | async-done | bytes 7712 | tf_op jit(solution)/shard_map/all_to_all | solution.py:31
  128.1 14.1 %all_to_all.30 = bf16[4,160,640]{2,1,0:T(8,128)(2,1)S(1)} all-to-all(bf16[4,160,640]{2,1,0:T(8,128)(2,1)S(1)} %pad_maximum_fusion.5), channel_id=1, replica_groups=mesh['z'=8,'x'=4,'y'=4,'c'=2] {'y'}, dimensions={0} | all-to-all | bytes 1638400 | tf_op jit(solution)/shard_map/all_to_all | solution.py:31
  142.2 2.3 %collective-permute-done.13 = bf16[4,160,640]{2,1,0:T(8,128)(2,1)S(1)} collective-permute-done((bf16[4,160,640]{2,1,0:T(8,128)(2,1)S(1)}, bf16[4,160,640]{2,1,0:T(8,128)(2,1)S(1)}, u32[]{:S(2)}, u32[]{:S(2)}) %collective-permute-start.13) | collective-permute-done | bytes 819232 | tf_op jit(solution)/shard_map/ppermute | solution.py:23
  145.4 2.1 %fusion.3 = (bf16[4,1,160,640]{3,2,1,0:T(8,128)(2,1)S(1)}, bf16[4,1,160,640]{3,2,1,0:T(8,128)(2,1)S(1)}) fusion(s32[]{:T(128)S(6)} %select_n.277, bf16[1,4,160,640]{3,2,1,0:T(8,128)(2,1)} %bitcast.76, bf16[1,4,160,640]{3,2,1,0:T(8,128)(2,1)} %bitcast.91, s32[]{:T(128)S(6)} %select_n.279), kind=kLoop, calls=%fused_computation.28 | loop fusion | flops 819200 | bytes 3276808 | tf_op jit(solution)/shard_map/stack | solution.py:199
  153.2 5.7 %collective-permute-start.20 = (bf16[64,1024]{1,0:T(8,128)(2,1)}, bf16[64,1024]{1,0:T(8,128)(2,1)}, u32[]{:S(2)}, u32[]{:S(2)}) collective-permute-start(bf16[64,1024]{1,0:T(8,128)(2,1)} %get-tuple-element.43), channel_id=1, source_target_pairs={{0,128},{32,160},{64,192},{96,224},{128,0},{160,32},{192,64},{224,... | collective-permute-start | bytes 393224 | tf_op jit(solution)/shard_map/ppermute | solution.py:23
  158.8 3.8 %collective-permute-start.18 = (bf16[64,1024]{1,0:T(8,128)(2,1)}, bf16[64,1024]{1,0:T(8,128)(2,1)}, u32[]{:S(2)}, u32[]{:S(2)}) collective-permute-start(bf16[64,1024]{1,0:T(8,128)(2,1)} %get-tuple-element.45), channel_id=1, source_target_pairs={{0,96},{32,128},{64,160},{96,192},{128,224},{160,0},{192,32},{224,... | collective-permute-start | bytes 393224 | tf_op jit(solution)/shard_map/ppermute | solution.py:23
  163.5 2.1 %collective-permute-start.16 = (bf16[64,1024]{1,0:T(8,128)(2,1)S(1)}, bf16[64,1024]{1,0:T(8,128)(2,1)}, u32[]{:S(2)}, u32[]{:S(2)}) collective-permute-start(bf16[64,1024]{1,0:T(8,128)(2,1)S(1)} %get-tuple-element.47), channel_id=1, source_target_pairs={{0,64},{32,96},{64,128},{96,160},{128,192},{160,224},{192,0},{224,... | collective-permute-start | bytes 393224 | tf_op jit(solution)/shard_map/ppermute | solution.py:23
  165.7 5.7 %collective-permute-start.15 = (bf16[64,1024]{1,0:T(8,128)(2,1)S(1)}, bf16[64,1024]{1,0:T(8,128)(2,1)S(1)}, u32[]{:S(2)}, u32[]{:S(2)}) collective-permute-start(bf16[64,1024]{1,0:T(8,128)(2,1)S(1)} %get-tuple-element.48), channel_id=1, source_target_pairs={{0,224},{32,0},{64,32},{96,64},{128,96},{160,128},{192,160},{224,1... | collective-permute-start | bytes 393224 | tf_op jit(solution)/shard_map/ppermute | solution.py:23
  171.4 3.3 %collective-permute-done.19 = bf16[64,1024]{1,0:T(8,128)(2,1)} collective-permute-done((bf16[64,1024]{1,0:T(8,128)(2,1)}, bf16[64,1024]{1,0:T(8,128)(2,1)}, u32[]{:S(2)}, u32[]{:S(2)}) %collective-permute-start.19) | collective-permute-done | bytes 131104 | tf_op jit(solution)/shard_map/ppermute | solution.py:23
  174.7 3.3 %collective-permute-start.14 = (bf16[64,1024]{1,0:T(8,128)(2,1)S(1)}, bf16[64,1024]{1,0:T(8,128)(2,1)S(1)}, u32[]{:S(2)}, u32[]{:S(2)}) collective-permute-start(bf16[64,1024]{1,0:T(8,128)(2,1)S(1)} %get-tuple-element.42), channel_id=1, source_target_pairs={{0,32},{32,64},{64,96},{96,128},{128,160},{160,192},{192,224},{224... | collective-permute-start | bytes 393224 | tf_op jit(solution)/shard_map/ppermute | solution.py:23
  179.6 5.4 %all-to-all-start.5 = ((bf16[32,2,1280]{2,1,0:T(2,128)(2,1)}), bf16[32,2,1280]{2,1,0:T(2,128)(2,1)S(1)}, u32[]{:S(2)}, u32[]{:S(2)}) async-start(bf16[32,2,1280]{2,1,0:T(2,128)(2,1)} %reshape.272), calls=%async_computation.5 | async-start | bytes 327680 | tf_op jit(solution)/shard_map/all_to_all | solution.py:31
  185.0 2.1 %convert_add_fusion.6 = f32[64,1024]{1,0:T(8,128)} fusion(bf16[64,1024]{1,0:T(8,128)(2,1)} %collective-permute-done.20, bf16[64,1024]{1,0:T(8,128)(2,1)} %collective-permute-done.19, bf16[64,1024]{1,0:T(8,128)(2,1)} %collective-permute-done.18, bf16[64,1024]{1,0:T(8,128)(2,1)} %collective-permute-done.17, bf16[64,1024]{1,0:T(8,128)(2,1)} %collective-permute-done.16, ...), kind=kLoop, calls=%fused_computation.59 | loop fusion | flops 917504 | bytes 1441796 | tf_op jit(solution)/shard_map/add | solution.py:215
  187.1 8.8 %all-to-all-done.5 = bf16[32,2,1280]{2,1,0:T(2,128)(2,1)S(1)} async-done(((bf16[32,2,1280]{2,1,0:T(2,128)(2,1)}), bf16[32,2,1280]{2,1,0:T(2,128)(2,1)S(1)}, u32[]{:S(2)}, u32[]{:S(2)}) %all-to-all-start.5) | async-done | bytes 163872 | tf_op jit(solution)/shard_map/all_to_all | solution.py:31
  (122 shorter events, 44.5 us)
Async XLA Ops:
  0.6 28.6 %copy-start = (bf16[2,160,2048]{2,1,0:T(8,128)(2,1)S(1)}, bf16[2,160,2048]{2,1,0:T(8,128)(2,1)}, u32[]{:S(2)}) copy-start(bf16[2,160,2048]{2,1,0:T(8,128)(2,1)} %param.15) | copy-start | bytes 3932164
  7.5 2.4 %collective-permute-start.3 = (bf16[320,1024]{1,0:T(8,128)(2,1)}, bf16[320,1024]{1,0:T(8,128)(2,1)S(1)}, u32[]{:S(2)}, u32[]{:S(2)}) collective-permute-start(bf16[320,1024]{1,0:T(8,128)(2,1)} %get-tuple-element.26), channel_id=1, source_target_pairs={{0,1},{1,0},{2,3},{3,2},{4,5},{5,4},{6,7},{7,6},{8,9},{9,8},{10,11... | collective-permute-start | bytes 1966088 | tf_op jit(solution)/shard_map/ppermute | solution.py:23
  7.5 6.7 %collective-permute-start.1 = (bf16[320,1024]{1,0:T(8,128)(2,1)}, bf16[320,1024]{1,0:T(8,128)(2,1)S(1)}, u32[]{:S(2)}, u32[]{:S(2)}) collective-permute-start(bf16[320,1024]{1,0:T(8,128)(2,1)} %get-tuple-element.22), channel_id=1, source_target_pairs={{0,1},{1,0},{2,3},{3,2},{4,5},{5,4},{6,7},{7,6},{8,9},{9,8},{10,11... | collective-permute-start | bytes 1966088 | tf_op jit(solution)/shard_map/ppermute | solution.py:23
  8.0 6.2 %collective-permute-start.2 = (bf16[320,1024]{1,0:T(8,128)(2,1)}, bf16[320,1024]{1,0:T(8,128)(2,1)S(1)}, u32[]{:S(2)}, u32[]{:S(2)}) collective-permute-start(bf16[320,1024]{1,0:T(8,128)(2,1)} %get-tuple-element.23), channel_id=1, source_target_pairs={{0,1},{1,0},{2,3},{3,2},{4,5},{5,4},{6,7},{7,6},{8,9},{9,8},{10,11... | collective-permute-start | bytes 1966088 | tf_op jit(solution)/shard_map/ppermute | solution.py:23
  12.2 10.1 %collective-permute-start.4 = (bf16[320,512]{1,0:T(8,128)(2,1)}, bf16[320,512]{1,0:T(8,128)(2,1)}, u32[]{:S(2)}, u32[]{:S(2)}) collective-permute-start(bf16[320,512]{1,0:T(8,128)(2,1)} %get-tuple-element.62), channel_id=1, source_target_pairs={{0,2},{2,4},{4,6},{6,0},{1,3},{3,5},{5,7},{7,1},{8,10},{10,12},{12... | collective-permute-start | bytes 983048 | tf_op jit(solution)/shard_map/ppermute | solution.py:23
  13.5 10.0 %collective-permute-start.5 = (bf16[320,512]{1,0:T(8,128)(2,1)}, bf16[320,512]{1,0:T(8,128)(2,1)}, u32[]{:S(2)}, u32[]{:S(2)}) collective-permute-start(bf16[320,512]{1,0:T(8,128)(2,1)} %get-tuple-element.61), channel_id=1, source_target_pairs={{0,6},{2,0},{4,2},{6,4},{1,7},{3,1},{5,3},{7,5},{8,14},{10,8},{12,... | collective-permute-start | bytes 983048 | tf_op jit(solution)/shard_map/ppermute | solution.py:23
  14.2 24.4 %collective-permute-start = (bf16[320,1024]{1,0:T(8,128)(2,1)}, bf16[320,1024]{1,0:T(8,128)(2,1)S(1)}, u32[]{:S(2)}, u32[]{:S(2)}) collective-permute-start(bf16[320,1024]{1,0:T(8,128)(2,1)} %get-tuple-element.21), channel_id=1, source_target_pairs={{0,1},{1,0},{2,3},{3,2},{4,5},{5,4},{6,7},{7,6},{8,9},{9,8},{10,11... | collective-permute-start | bytes 1966088 | tf_op jit(solution)/shard_map/ppermute | solution.py:23
  23.4 6.1 %copy-start.12 = (bf16[64,1024]{1,0:T(8,128)(2,1)S(1)}, bf16[64,1024]{1,0:T(8,128)(2,1)}, u32[]{:S(2)}) copy-start(bf16[64,1024]{1,0:T(8,128)(2,1)} %param.13) | copy-start | bytes 393220
  26.3 17.2 %collective-permute-start.7 = (bf16[320,1024]{1,0:T(8,128)(2,1)}, bf16[320,1024]{1,0:T(8,128)(2,1)}, u32[]{:S(2)}, u32[]{:S(2)}) collective-permute-start(bf16[320,1024]{1,0:T(8,128)(2,1)} %get-tuple-element.34), channel_id=1, source_target_pairs={{0,6},{2,0},{4,2},{6,4},{1,7},{3,1},{5,3},{7,5},{8,14},{10,8},{12,... | collective-permute-start | bytes 1966088 | tf_op jit(solution)/shard_map/ppermute | solution.py:23
  26.8 16.7 %collective-permute-start.6 = (bf16[320,1024]{1,0:T(8,128)(2,1)}, bf16[320,1024]{1,0:T(8,128)(2,1)}, u32[]{:S(2)}, u32[]{:S(2)}) collective-permute-start(bf16[320,1024]{1,0:T(8,128)(2,1)} %get-tuple-element.33), channel_id=1, source_target_pairs={{0,2},{2,4},{4,6},{6,0},{1,3},{3,5},{5,7},{7,1},{8,10},{10,12},{12... | collective-permute-start | bytes 1966088 | tf_op jit(solution)/shard_map/ppermute | solution.py:23
  30.9 7.5 %copy-start.15 = (s32[2,32]{1,0:T(2,128)S(1)}, s32[2,32]{1,0:T(2,128)}, u32[]{:S(2)}) copy-start(s32[2,32]{1,0:T(2,128)} %param.11) | copy-start | bytes 772
  30.9 7.7 %copy-start.14 = (s32[2,160]{1,0:T(2,128)S(1)}, s32[2,160]{1,0:T(2,128)}, u32[]{:S(2)}) copy-start(s32[2,160]{1,0:T(2,128)} %param.12) | copy-start | bytes 3844
  30.9 43.3 %all-to-all-start = ((bf16[8,80,1024]{2,1,0:T(8,128)(2,1)}), bf16[8,80,1024]{2,1,0:T(8,128)(2,1)S(1)}, u32[]{:S(2)}, u32[]{:S(2)}) async-start(bf16[8,80,1024]{2,1,0:T(8,128)(2,1)} %pad_maximum_fusion.4), calls=%async_computation | async-start | bytes 2621440 | tf_op jit(solution)/shard_map/all_to_all | solution.py:31
  45.8 18.3 %copy-start.2 = (f32[2,160,1024]{2,1,0:T(8,128)}, f32[2,160,1024]{2,1,0:T(8,128)S(1)}, u32[]{:S(2)}) copy-start(f32[2,160,1024]{2,1,0:T(8,128)S(1)} %convert_add_fusion.1) | copy-start | bytes 3932164
  46.1 16.2 %collective-permute-start.10 = (bf16[2,160,1024]{2,1,0:T(8,128)(2,1)S(1)}, bf16[2,160,1024]{2,1,0:T(8,128)(2,1)S(1)}, u32[]{:S(2)}, u32[]{:S(2)}) collective-permute-start(bf16[2,160,1024]{2,1,0:T(8,128)(2,1)S(1)} %convolution_convert_fusion.2), channel_id=1, source_target_pairs={{0,8},{8,16},{16,24},{24,0},{1,9},{9,17},{17,25},{25,1},{2,10},{10... | collective-permute-start | bytes 1966088 | tf_op jit(solution)/shard_map/ppermute | solution.py:23
  47.7 15.6 %collective-permute-start.8 = (bf16[2,160,1024]{2,1,0:T(8,128)(2,1)S(1)}, bf16[2,160,1024]{2,1,0:T(8,128)(2,1)S(1)}, u32[]{:S(2)}, u32[]{:S(2)}) collective-permute-start(bf16[2,160,1024]{2,1,0:T(8,128)(2,1)S(1)} %convolution_convert_fusion.2), channel_id=1, source_target_pairs={{0,24},{8,0},{16,8},{24,16},{1,25},{9,1},{17,9},{25,17},{2,26},{10... | collective-permute-start | bytes 1966088 | tf_op jit(solution)/shard_map/ppermute | solution.py:23
  63.1 8.6 %collective-permute-start.11 = (bf16[1,160,1024]{2,1,0:T(8,128)(2,1)}, bf16[1,160,1024]{2,1,0:T(8,128)(2,1)}, u32[]{:S(2)}, u32[]{:S(2)}) collective-permute-start(bf16[1,160,1024]{2,1,0:T(8,128)(2,1)} %slice.75), channel_id=1, source_target_pairs={{0,8},{8,16},{16,24},{24,0},{1,9},{9,17},{17,25},{25,1},{2,10},{10... | collective-permute-start | bytes 983048 | tf_op jit(solution)/shard_map/ppermute | solution.py:23
  64.2 8.0 %collective-permute-start.9 = (bf16[1,160,1024]{2,1,0:T(8,128)(2,1)}, bf16[1,160,1024]{2,1,0:T(8,128)(2,1)}, u32[]{:S(2)}, u32[]{:S(2)}) collective-permute-start(bf16[1,160,1024]{2,1,0:T(8,128)(2,1)} %slice.74), channel_id=1, source_target_pairs={{0,24},{8,0},{16,8},{24,16},{1,25},{9,1},{17,9},{25,17},{2,26},{10... | collective-permute-start | bytes 983048 | tf_op jit(solution)/shard_map/ppermute | solution.py:23
  79.6 11.6 %all-to-all-start.1 = ((bf16[4,64,512]{2,1,0:T(8,128)(2,1)}), bf16[4,64,512]{2,1,0:T(8,128)(2,1)S(1)}, u32[]{:S(2)}, u32[]{:S(2)}) async-start(bf16[4,64,512]{2,1,0:T(8,128)(2,1)} %reshape.249), calls=%async_computation.1 | async-start | bytes 524288 | tf_op jit(solution)/shard_map/all_to_all | solution.py:31
  95.9 2.4 %collective-permute-start.12 = (bf16[4,160,512]{2,1,0:T(8,128)(2,1)}, bf16[4,160,512]{2,1,0:T(8,128)(2,1)}, u32[]{:S(2)}, u32[]{:S(2)}) collective-permute-start(bf16[4,160,512]{2,1,0:T(8,128)(2,1)} %dynamic-slice_bitcast_fusion), channel_id=1, source_target_pairs={{0,1},{1,0},{2,3},{3,2},{4,5},{5,4},{6,7},{7,6},{8,9},{9,8},{10,11... | collective-permute-start | bytes 1966088 | tf_op jit(solution)/shard_map/ppermute | solution.py:23
  99.7 8.6 %copy-start.13 = (f32[2048]{0:T(1024)S(1)}, f32[2048]{0:T(1024)}, u32[]{:S(2)}) copy-start(f32[2048]{0:T(1024)} %param.14) | copy-start | bytes 24580
  100.6 16.1 %all-to-all-start.2 = ((bf16[4,160,512]{2,1,0:T(8,128)(2,1)}), bf16[4,160,512]{2,1,0:T(8,128)(2,1)S(1)}, u32[]{:S(2)}, u32[]{:S(2)}) async-start(bf16[4,160,512]{2,1,0:T(8,128)(2,1)} %pad_maximum_fusion.6), calls=%async_computation.2 | async-start | bytes 1310720 | tf_op jit(solution)/shard_map/all_to_all | solution.py:31
  117.8 8.5 %all-to-all-start.3 = ((f32[4,1,480]{2,1,0:T(1,128)}), f32[4,1,480]{2,1,0:T(1,128)S(1)}, u32[]{:S(2)}, u32[]{:S(2)}) async-start(f32[4,1,480]{2,1,0:T(1,128)} %reshape.270), calls=%async_computation.3 | async-start | bytes 16384 | tf_op jit(solution)/shard_map/all_to_all | solution.py:31
  142.2 2.3 %collective-permute-start.13 = (bf16[4,160,640]{2,1,0:T(8,128)(2,1)S(1)}, bf16[4,160,640]{2,1,0:T(8,128)(2,1)S(1)}, u32[]{:S(2)}, u32[]{:S(2)}) collective-permute-start(bf16[4,160,640]{2,1,0:T(8,128)(2,1)S(1)} %all_to_all.30), channel_id=1, source_target_pairs={{0,1},{1,0},{2,3},{3,2},{4,5},{5,4},{6,7},{7,6},{8,9},{9,8},{10,11... | collective-permute-start | bytes 2457608 | tf_op jit(solution)/shard_map/ppermute | solution.py:23
  153.2 12.5 %collective-permute-start.20 = (bf16[64,1024]{1,0:T(8,128)(2,1)}, bf16[64,1024]{1,0:T(8,128)(2,1)}, u32[]{:S(2)}, u32[]{:S(2)}) collective-permute-start(bf16[64,1024]{1,0:T(8,128)(2,1)} %get-tuple-element.43), channel_id=1, source_target_pairs={{0,128},{32,160},{64,192},{96,224},{128,0},{160,32},{192,64},{224,... | collective-permute-start | bytes 393224 | tf_op jit(solution)/shard_map/ppermute | solution.py:23
  158.8 15.8 %collective-permute-start.19 = (bf16[64,1024]{1,0:T(8,128)(2,1)}, bf16[64,1024]{1,0:T(8,128)(2,1)}, u32[]{:S(2)}, u32[]{:S(2)}) collective-permute-start(bf16[64,1024]{1,0:T(8,128)(2,1)} %get-tuple-element.44), channel_id=1, source_target_pairs={{0,160},{32,192},{64,224},{96,0},{128,32},{160,64},{192,96},{224,1... | collective-permute-start | bytes 393224 | tf_op jit(solution)/shard_map/ppermute | solution.py:23
  158.8 26.1 %collective-permute-start.18 = (bf16[64,1024]{1,0:T(8,128)(2,1)}, bf16[64,1024]{1,0:T(8,128)(2,1)}, u32[]{:S(2)}, u32[]{:S(2)}) collective-permute-start(bf16[64,1024]{1,0:T(8,128)(2,1)} %get-tuple-element.45), channel_id=1, source_target_pairs={{0,96},{32,128},{64,160},{96,192},{128,224},{160,0},{192,32},{224,... | collective-permute-start | bytes 393224 | tf_op jit(solution)/shard_map/ppermute | solution.py:23
  162.7 22.3 %collective-permute-start.17 = (bf16[64,1024]{1,0:T(8,128)(2,1)S(1)}, bf16[64,1024]{1,0:T(8,128)(2,1)}, u32[]{:S(2)}, u32[]{:S(2)}) collective-permute-start(bf16[64,1024]{1,0:T(8,128)(2,1)S(1)} %get-tuple-element.46), channel_id=1, source_target_pairs={{0,192},{32,224},{64,0},{96,32},{128,64},{160,96},{192,128},{224,1... | collective-permute-start | bytes 393224 | tf_op jit(solution)/shard_map/ppermute | solution.py:23
  163.5 21.5 %collective-permute-start.16 = (bf16[64,1024]{1,0:T(8,128)(2,1)S(1)}, bf16[64,1024]{1,0:T(8,128)(2,1)}, u32[]{:S(2)}, u32[]{:S(2)}) collective-permute-start(bf16[64,1024]{1,0:T(8,128)(2,1)S(1)} %get-tuple-element.47), channel_id=1, source_target_pairs={{0,64},{32,96},{64,128},{96,160},{128,192},{160,224},{192,0},{224,... | collective-permute-start | bytes 393224 | tf_op jit(solution)/shard_map/ppermute | solution.py:23
  165.7 19.3 %collective-permute-start.15 = (bf16[64,1024]{1,0:T(8,128)(2,1)S(1)}, bf16[64,1024]{1,0:T(8,128)(2,1)S(1)}, u32[]{:S(2)}, u32[]{:S(2)}) collective-permute-start(bf16[64,1024]{1,0:T(8,128)(2,1)S(1)} %get-tuple-element.48), channel_id=1, source_target_pairs={{0,224},{32,0},{64,32},{96,64},{128,96},{160,128},{192,160},{224,1... | collective-permute-start | bytes 393224 | tf_op jit(solution)/shard_map/ppermute | solution.py:23
  174.7 10.3 %collective-permute-start.14 = (bf16[64,1024]{1,0:T(8,128)(2,1)S(1)}, bf16[64,1024]{1,0:T(8,128)(2,1)S(1)}, u32[]{:S(2)}, u32[]{:S(2)}) collective-permute-start(bf16[64,1024]{1,0:T(8,128)(2,1)S(1)} %get-tuple-element.42), channel_id=1, source_target_pairs={{0,32},{32,64},{64,96},{96,128},{128,160},{160,192},{192,224},{224... | collective-permute-start | bytes 393224 | tf_op jit(solution)/shard_map/ppermute | solution.py:23
  179.6 16.3 %all-to-all-start.5 = ((bf16[32,2,1280]{2,1,0:T(2,128)(2,1)}), bf16[32,2,1280]{2,1,0:T(2,128)(2,1)S(1)}, u32[]{:S(2)}, u32[]{:S(2)}) async-start(bf16[32,2,1280]{2,1,0:T(2,128)(2,1)} %reshape.272), calls=%async_computation.5 | async-start | bytes 327680 | tf_op jit(solution)/shard_map/all_to_all | solution.py:31
  (10 other events, 12.8 us)

commit v2 on v1

v2 whole, which is shorter than its diff:
```python
import functools
import math

import jax
import jax.numpy as jnp
from jax import lax
from jax.experimental import pallas as pl
from jax.experimental.pallas import tpu as pltpu
from jax.sharding import Mesh, PartitionSpec as P


K = 5
STEPS = 2
NZ, NX, NY, NC = 8, 4, 4, 2
EPSILON = 1e-06
BF16 = jnp.bfloat16
F32 = jnp.float32
VMEM = pl.BlockSpec(memory_space=pltpu.VMEM)
SMEM = pl.BlockSpec(memory_space=pltpu.SMEM)


def shift(value, axis, size, by):
    return lax.ppermute(value, axis, [(i, (i + by) % size) for i in range(size)])


def swap(value):
    return shift(value, "c", NC, 1)


def exchange(value, axis):
    return lax.all_to_all(value, axis, 0, 0, tiled=True)


def take(value, index, axis=0):
    return lax.dynamic_index_in_dim(value, index, axis, False)


def project_kernel(blocks, split, adds, ctx_ref, weight_ref, *refs):
    added, outs, (held, sems) = refs[:adds], list(refs[adds:-2]), refs[-2:]
    rows, width = ctx_ref.shape[0], held.shape[2]
    y, c = lax.axis_index("y"), lax.axis_index("c")
    copies = []
    for i, (d, other) in enumerate(blocks):
        block = lax.rem(y + d, NY) * NC + (1 - c if other else c)
        span = pl.ds(pl.multiple_of(block * width, width), width)
        copies.append(pltpu.make_async_copy(weight_ref.at[:, span], held.at[i], sems.at[i]))
        copies[-1].start()
    for i in range(len(blocks)):
        copies[i].wait()
        tile = width // 2

        @pl.loop(0, width // tile)
        def _(t):
            span = pl.ds(pl.multiple_of(t * tile, tile), tile)
            product = jnp.dot(ctx_ref[...], held[i, :, span], preferred_element_type=F32)
            if i < adds:
                product = product + added[i][:, span].astype(F32)
            for s in range(split):
                step = rows // split
                outs[i * split + s][:, span] = product[s * step:(s + 1) * step].astype(BF16)


def project(blocks, ctx, weight, width, added=(), split=1):
    count, (rows, depth) = len(blocks), ctx.shape
    return pl.pallas_call(
        functools.partial(project_kernel, blocks, split, len(added)),
        in_specs=[VMEM, pl.BlockSpec(memory_space=pl.ANY)] + [VMEM] * len(added),
        out_specs=[VMEM] * (count * split),
        out_shape=[jax.ShapeDtypeStruct((rows // split, width), BF16)] * (count * split),
        scratch_shapes=[
            pltpu.VMEM((count, depth, width), weight.dtype),
            pltpu.SemaphoreType.DMA((count,)),
        ],
        cost_estimate=pl.CostEstimate(
            flops=2 * count * rows * depth * width,
            bytes_accessed=2 * count * (depth + rows) * width,
            transcendentals=0,
        ),
        name="project",
    )(ctx, weight, *added)


def local(context, o_weight, residual, counts, slots, fc_weight, gain, goal):
    z, x, y, c = (lax.axis_index(name) for name in ("z", "x", "y", "c"))
    rows = context.shape[1]
    width = residual.shape[2]
    per_peer = rows // (NZ * NX)
    feats = fc_weight.shape[0]
    some = NZ * feats
    draft_width = gain.shape[0]
    weight = 1.0 / math.sqrt(STEPS * rows * NZ * NX)

    ctx = context.reshape(STEPS * rows, context.shape[2])
    first, far_own, one, three = project(
        ((2, True), (2, False), (1, True), (3, True)), ctx, o_weight, width
    )
    first, one, three = swap(first), swap(one), swap(three)
    far = (far_own.astype(F32) + first.astype(F32)).astype(BF16).reshape(STEPS, rows, width)
    *near, zero_0, zero_1, own_0, own_1 = project(
        ((1, False), (3, False), (0, True), (0, False)), ctx, o_weight, width, (one, three), STEPS
    )
    own, zero = (own_0, own_1), [swap(v) for v in (zero_0, zero_1)]

    totals = []
    for s in range(STEPS):
        total = shift(far[s], "y", NY, 2).astype(F32)
        total = total + shift(near[s], "y", NY, 1).astype(F32)
        total = total + shift(near[STEPS + s], "y", NY, -1).astype(F32)
        totals.append(total + own[s].astype(F32) + zero[s].astype(F32))
    states = [residual[s].astype(F32) + totals[s] for s in range(STEPS)]
    verified = jnp.stack(states)

    slot = per_peer + -per_peer % 8
    chosen = jnp.arange(NZ * slot, dtype=jnp.int32)
    chosen = jnp.where(chosen % slot < per_peer, (chosen // slot * NX + y) * per_peer + chosen % slot, -1)
    chosen = (chosen[:, None] == jnp.arange(rows, dtype=jnp.int32)).astype(BF16)
    target = jnp.dot(chosen, take(goal, c), preferred_element_type=F32).astype(BF16)
    cuts = [target[:, i:i + width].reshape(NZ, slot, width) for i in range(0, draft_width, width)]
    load = jnp.concatenate([jnp.broadcast_to(fc_weight, (NZ, feats, width)), *cuts], 1)
    load = exchange(load, "z")
    fc_all = load[:, :feats].reshape(some, width)
    cuts = [load[:, feats + i * slot:feats + (i + 1) * slot] for i in range(draft_width // width)]
    target = jnp.concatenate(cuts, 2).reshape(NZ * slot, NZ, NX, feats).transpose(2, 0, 1, 3)
    target = target.reshape(NX, NZ * slot, some)
    pieces = [take(target, x)]
    for m in range(1, NX):
        piece = take(target, (x + m) % NX)
        pieces.append(shift(piece, "x", NX, m))
    target = jnp.concatenate(pieces, 0)
    packed = jnp.arange(rows, dtype=jnp.int32)
    peer = packed // per_peer
    packed = ((x + NX - peer % NX) % NX * NZ + peer // NX) * slot + packed % per_peer
    packed = packed[:, None] == jnp.arange(target.shape[0], dtype=jnp.int32)
    target = jnp.dot(packed.astype(BF16), target, preferred_element_type=F32)

    source = z * NX + x
    position = slots // rows * per_peer + slots % rows - source * per_peer
    accepted = jnp.arange(rows, dtype=jnp.int32) % K < jnp.repeat(counts, K, axis=1)
    position = jnp.where(accepted, position, -1)
    pick = (position[:, None, :] == jnp.arange(rows, dtype=jnp.int32)[None, :, None]).astype(BF16)

    trained, partial = [], []
    for s in range(STEPS):
        mine = jnp.dot(pick[s], states[s].astype(BF16), preferred_element_type=F32).astype(BF16)
        mine = lax.optimization_barrier(mine)
        around = [mine] + [shift(mine, "x", NX, -m) for m in range(1, NX)]
        trained.append(jnp.concatenate(around, 0))
        product = lax.dot_general(
            trained[s], fc_all, (((1,), (1,)), ((), ())), preferred_element_type=F32
        ).astype(BF16)
        partial.append(lax.optimization_barrier(product) if s == 0 else product)

    given = swap(jnp.where(c == 0, partial[1], partial[0])).reshape(NX, rows, some)
    kept = jnp.where(c == 0, partial[0], partial[1]).reshape(NX, rows, some)

    def term(i):
        m = (i - x + NX) % NX
        return (take(kept, m).astype(F32) + take(given, m).astype(F32)).astype(BF16)

    summed = jnp.stack([term(i) for i in range(NY)])
    summed = exchange(summed, "y").astype(F32).sum(0)

    scale = take(gain.reshape(NZ, NX, feats), x, 1).reshape(1, some)
    scaled = summed * scale
    sums = jnp.stack(
        [jnp.sum(summed * summed, -1), jnp.sum(scaled * scaled, -1), jnp.sum(scaled * target, -1)]
    )
    sums = sums + shift(sums, "x", NX, 2) + shift(sums, "x", NX, 1) + shift(sums, "x", NX, 3)
    mean_square, gained, aimed = sums[0] / draft_width, sums[1] / draft_width, sums[2] / draft_width
    inverse = lax.rsqrt(mean_square + EPSILON)[:, None]
    spread = weight * (inverse * gained[:, None] - aimed[:, None])
    normed = summed * inverse * scale
    pulled = scale * (weight * (normed - target))
    back = (inverse * (pulled - summed * (inverse * inverse) * spread)).astype(BF16)

    normed = normed.astype(BF16)
    pair = NC * feats
    load = jnp.stack([jnp.concatenate([back, normed[:, i * pair:(i + 1) * pair]], 1) for i in range(NY)])
    load = exchange(load, "y")
    both = jnp.stack([load, swap(load)])
    both = jnp.stack([take(both, (s + c) % NC) for s in range(NC)])
    lined = jnp.stack([take(both, (m + x) % NX, 1) for m in range(NX)], 1)

    def term(s):
        return lax.dot_general(
            lined[s, :, :, :some].reshape(NX * rows, some),
            trained[s],
            (((0,), (0,)), ((), ())),
            preferred_element_type=F32,
        )

    terms = term(0) + term(1)

    def block(m):
        return lax.dynamic_slice_in_dim(terms, (z + m) % NZ * feats, feats, 0)

    grad = block(0)
    arrived = {}
    for m in (4, 3, 5, 2, 6, 1):
        arrived[m] = shift(block(m).astype(BF16), "z", NZ, m)
    for m in (7,):
        arrived[m] = shift(block(m).astype(BF16), "z", NZ, m)
    for m in (1, 7, 2, 6, 3, 5, 4):
        grad = grad + arrived[m].astype(F32)

    out = lax.dynamic_slice_in_dim(both[:, :, :, some:], c * feats, feats, 3)
    out = out.reshape(STEPS * NX, NZ * NX, per_peer, feats).transpose(1, 0, 2, 3)
    out = exchange(out.reshape(NZ * NX, NX * STEPS * per_peer, feats), ("z", "x"))
    out = out.reshape(NZ, NX, STEPS, NX, per_peer, feats).transpose(2, 0, 3, 4, 1, 5)
    draft_out = out.reshape(STEPS, rows, NX * feats).astype(F32)
    return verified, draft_out, grad


def solution(mesh):
    grid = Mesh(mesh.devices.reshape(NZ, NX, NY, NC), ("z", "x", "y", "c"))
    r, t = ("z", "x"), ("y", "c")
    placed = (
        P(None, r, t),
        P(t, None),
        P(None, r, t),
        P(None, r),
        P(None, r),
        P(r, t),
        P(),
        P(None, r, None),
    )

    return jax.shard_map(
        local,
        mesh=grid,
        in_specs=placed,
        out_specs=(P(None, r, t), P(None, r, t), P(r, t)),
        check_vma=False,
    )
```

time: 200 us -> 191 us (0.955)
  waiting for transfers between devices: 55.2 us -> 36.7 us
  starting transfers between devices: 62.4 us -> 79.8 us
  local copies, waits for them, and re-layouts: 21.1 us -> 11.3 us
  matrix products: 5.96 us -> 13.1 us
  Pallas kernels: 17.6 us -> 12.8 us
    all_to_all x5 -> x3, waiting for transfers between devices: 24.6 us -> 2.7 us  [exchange(): return lax.all_to_all(value, axis, 0, 0, tiled=True)]
    ppermute x21 -> x32, starting transfers between devices: 33.7 us -> 53.8 us  [shift(): lax.ppermute(value, axis, [(i, (i + by) % size) for i in range(size)])]
    dot_general x3 -> x6, matrix products: 5.44 us -> 12.5 us  [the longest x2 4.46 us: term(): lax.dot_general(lined[s, :, :, :some].reshape(NX * rows, some), trained[s...]
    pallas_call x4 -> x2, Pallas kernels: 17.6 us -> 12.8 us  [project(): pl.pallas_call(functools.partial(project_kernel, blocks, split, len(added...]
    ppermute x21 -> x32, waiting for transfers between devices: 30.5 us -> 34 us  [shift(): lax.ppermute(value, axis, [(i, (i + by) % size) for i in range(size)])]
    unnamed x37 -> x43, local copies, waits for them, and re-layouts: 8.54 us -> 5.64 us
    all_to_all x5 -> x3, starting transfers between devices: 28.7 us -> 26 us  [exchange(): return lax.all_to_all(value, axis, 0, 0, tiled=True)]
    add x3 -> x2, other arithmetic: 2.25 us -> 0.04 us  [the longest x1 0.03 us: local(): ((x + NX - peer % NX) % NX * NZ + peer // NX) * slot + packed % per_peer]
  transfers between devices with their start and end apart: 26 -> 35, of which waited for: 13 -> 14; matrix products, arithmetic and copies ran while one was open for 9% -> 13% of each run, Pallas kernels for 6% -> 3%
where the time goes in v2:
time: 191 us; the launch traced here: 187 us
  starting transfers between devices  79.8 us (42%)
  waiting for transfers between devices  36.7 us (19%)
  other arithmetic  18.4 us (10%)
  blocking collectives  13.7 us (7%)
  matrix products  13.1 us (7%)
  Pallas kernels  12.8 us (7%)
  local copies, waits for them, and re-layouts  11.3 us (6%)
    ppermute x32, starting transfers between devices, shift(): lax.ppermute(value, axis, [(i, (i + by) % size) for i in range(size)])  53.8 us
    ppermute x32, waiting for transfers between devices, shift(): lax.ppermute(value, axis, [(i, (i + by) % size) for i in range(size)])  34 us
    all_to_all x3, starting transfers between devices, exchange(): return lax.all_to_all(value, axis, 0, 0, tiled=True)  26 us
    all_to_all x1, blocking collectives, exchange(): return lax.all_to_all(value, axis, 0, 0, tiled=True)  13.7 us
    pallas_call x2, Pallas kernels, project(): pl.pallas_call(functools.partial(project_kernel, blocks, split, len(added...  12.8 us
    another operation x2, other arithmetic, local(): verified = jnp.stack(states)  6.05 us
    unnamed x43, local copies, waits for them, and re-layouts  5.64 us
    dot_general x2, matrix products, term(): lax.dot_general(lined[s, :, :, :some].reshape(NX * rows, some), trained[s...  4.46 us
  transfers between devices with their start and end apart: 35, of which 14 were waited for; matrix products, arithmetic and copies ran while one was open for 13% of the time, Pallas kernels for 3%

profile of v2, /device:TPU:16, one launch (start us, length us, event | category | flops | bytes accessed | tf_op | source)
XLA Modules:
  0.0 186.9 jit_solution(3750946051124788267)
XLA Ops:
  0.6 6.2 %project.2 = (bf16[320,1024]{1,0:T(8,128)(2,1)}, bf16[320,1024]{1,0:T(8,128)(2,1)}, bf16[320,1024]{1,0:T(8,128)(2,1)}, bf16[320,1024]{1,0:T(8,128)(2,1)}) custom-call(bf16[320,512]{1,0:T(8,128)(2,1)} %bitcast.84, bf16[512,8192]{1,0:T(8,128)(2,1)} %weight_ref.3), custom_call_target="tpu_custom_call" | custom-call | flops 1342177280 | bytes 6815744 | tf_op jit(solution)/shard_map/project/pallas_call | solution.py:65
  9.1 8.6 %all-to-all-start = ((bf16[8,80,1024]{2,1,0:T(8,128)(2,1)}), bf16[8,80,1024]{2,1,0:T(8,128)(2,1)S(1)}, u32[]{:S(2)}, u32[]{:S(2)}) async-start(bf16[8,80,1024]{2,1,0:T(8,128)(2,1)} %pad_maximum_fusion.2), calls=%async_computation | async-start | bytes 2621440 | tf_op jit(solution)/shard_map/all_to_all | solution.py:31
  18.8 6.5 %project.3 = (bf16[160,1024]{1,0:T(8,128)(2,1)}, bf16[160,1024]{1,0:T(8,128)(2,1)}, bf16[160,1024]{1,0:T(8,128)(2,1)}, bf16[160,1024]{1,0:T(8,128)(2,1)}, bf16[1...) custom-call(bf16[320,512]{1,0:T(8,128)(2,1)} %bitcast.85, ...), custom_call_target="tpu_custom_call" | custom-call | flops 1342177280 | bytes 6815744 | tf_op jit(solution)/shard_map/project/pallas_call | solution.py:65
  31.9 2.7 %collective-permute-start.9 = (bf16[160,1024]{1,0:T(8,128)(2,1)S(1)}, bf16[160,1024]{1,0:T(8,128)(2,1)S(1)}, u32[]{:S(2)}, u32[]{:S(2)}) collective-permute-start(bf16[160,1024]{1,0:T(8,128)(2,1)S(1)} %copy-done.18), channel_id=1, source_target_pairs={{0,6},{2,0},{4,2},{6,4},{1,7},{3,1},{5,3},{7,5},{8,14},{10,8},{12,... | collective-permute-start | bytes 983048 | tf_op jit(solution)/shard_map/ppermute | solution.py:23
  34.6 2.1 %collective-permute-done.5 = bf16[160,1024]{1,0:T(8,128)(2,1)S(1)} collective-permute-done((bf16[160,1024]{1,0:T(8,128)(2,1)}, bf16[160,1024]{1,0:T(8,128)(2,1)S(1)}, u32[]{:S(2)}, u32[]{:S(2)}) %collective-permute-start.5) | collective-permute-done | bytes 327712 | tf_op jit(solution)/shard_map/ppermute | solution.py:23
  36.7 9.5 %collective-permute-start.8 = (bf16[160,1024]{1,0:T(8,128)(2,1)}, bf16[160,1024]{1,0:T(8,128)(2,1)}, u32[]{:S(2)}, u32[]{:S(2)}) collective-permute-start(bf16[160,1024]{1,0:T(8,128)(2,1)} %get-tuple-element.23), channel_id=1, source_target_pairs={{0,2},{2,4},{4,6},{6,0},{1,3},{3,5},{5,7},{7,1},{8,10},{10,12},{12... | collective-permute-start | bytes 983048 | tf_op jit(solution)/shard_map/ppermute | solution.py:23
  49.9 2.8 %collective-permute-start.12 = (bf16[160,1024]{1,0:T(8,128)(2,1)}, bf16[160,1024]{1,0:T(8,128)(2,1)}, u32[]{:S(2)}, u32[]{:S(2)}) collective-permute-start(bf16[160,1024]{1,0:T(8,128)(2,1)} %convolution_convert_fusion.4), channel_id=1, source_target_pairs={{0,16},{8,24},{16,0},{24,8},{1,17},{9,25},{17,1},{25,9},{2,18},{10... | collective-permute-start | bytes 983048 | tf_op jit(solution)/shard_map/ppermute | solution.py:23
  54.9 3.6 %collective-permute-done.7 = bf16[160,1024]{1,0:T(8,128)(2,1)} collective-permute-done((bf16[160,1024]{1,0:T(8,128)(2,1)}, bf16[160,1024]{1,0:T(8,128)(2,1)}, u32[]{:S(2)}, u32[]{:S(2)}) %collective-permute-start.7) | collective-permute-done | bytes 327712 | tf_op jit(solution)/shard_map/ppermute | solution.py:23
  58.5 2.5 %convolution_convert_fusion.3 = bf16[160,1024]{1,0:T(8,128)(2,1)} fusion(pred[2,160,160]{2,1,0:T(32,128)(4,1)S(1)} %iota_compare_fusion, bf16[160,1024]{1,0:T(8,128)(2,1)} %copy-done.9, bf16[160,1024]{1,0:T(8,128)(2,1)} %get-tuple-element.25, bf16[160,1024]{1,0:T(8,128)(2,1)} %copy-done.10, bf16[160,1024]{1,0:T(8,128)(2,1)} %collective-permute-done.8, ...), kind=kOutput, calls=%fused_computation.24 | convolution fusion | flops 54558720 | bytes 2334720 | tf_op jit(solution)/shard_map/dot_general | solution.py:144
  62.5 2.7 %collective-permute-start.15 = (bf16[160,1024]{1,0:T(8,128)(2,1)}, bf16[160,1024]{1,0:T(8,128)(2,1)}, u32[]{:S(2)}, u32[]{:S(2)}) collective-permute-start(bf16[160,1024]{1,0:T(8,128)(2,1)} %convolution_convert_fusion.3), channel_id=1, source_target_pairs={{0,16},{8,24},{16,0},{24,8},{1,17},{9,25},{17,1},{25,9},{2,18},{10... | collective-permute-start | bytes 983048 | tf_op jit(solution)/shard_map/ppermute | solution.py:23
  66.9 2.6 %collective-permute-done.11 = bf16[160,1024]{1,0:T(8,128)(2,1)} collective-permute-done((bf16[160,1024]{1,0:T(8,128)(2,1)}, bf16[160,1024]{1,0:T(8,128)(2,1)}, u32[]{:S(2)}, u32[]{:S(2)}) %collective-permute-start.11) | collective-permute-done | bytes 327712 | tf_op jit(solution)/shard_map/ppermute | solution.py:23
  69.5 2.2 %convolution_convert_fusion.2 = bf16[640,512]{1,0:T(8,128)(2,1)S(1)} fusion(bf16[512,1024]{1,0:T(8,128)(2,1)S(1)} %bitcast.88, bf16[160,1024]{1,0:T(8,128)(2,1)} %collective-permute-done.13, bf16[160,1024]{1,0:T(8,128)(2,1)} %collective-permute-done.12, bf16[160,1024]{1,0:T(8,128)(2,1)} %collective-permute-done.11, ...), kind=kOutput, calls=%fused_computation.17 | convolution fusion | flops 676659200 | bytes 3014656 | tf_op jit(solution)/shard_map/dot_general | solution.py:148
  71.7 2.5 %collective-permute-done.16 = bf16[160,1024]{1,0:T(8,128)(2,1)} collective-permute-done((bf16[160,1024]{1,0:T(8,128)(2,1)}, bf16[160,1024]{1,0:T(8,128)(2,1)}, u32[]{:S(2)}, u32[]{:S(2)}) %collective-permute-start.16) | collective-permute-done | bytes 327712 | tf_op jit(solution)/shard_map/ppermute | solution.py:23
  74.1 4.1 %collective-permute-done.15 = bf16[160,1024]{1,0:T(8,128)(2,1)} collective-permute-done((bf16[160,1024]{1,0:T(8,128)(2,1)}, bf16[160,1024]{1,0:T(8,128)(2,1)}, u32[]{:S(2)}, u32[]{:S(2)}) %collective-permute-start.15) | collective-permute-done | bytes 327712 | tf_op jit(solution)/shard_map/ppermute | solution.py:23
  78.2 2.2 %convolution_convert_fusion.1 = bf16[640,512]{1,0:T(8,128)(2,1)S(1)} fusion(bf16[512,1024]{1,0:T(8,128)(2,1)S(1)} %bitcast.89, bf16[160,1024]{1,0:T(8,128)(2,1)} %collective-permute-done.16, bf16[160,1024]{1,0:T(8,128)(2,1)} %collective-permute-done.15, bf16[160,1024]{1,0:T(8,128)(2,1)S(1)} %collective-permute-done.14, ...), kind=kOutput, calls=%fused_computation.16 | convolution fusion | flops 676659200 | bytes 3014656 | tf_op jit(solution)/shard_map/dot_general | solution.py:148
  81.8 2.2 %collective-permute-done.17 = bf16[640,512]{1,0:T(8,128)(2,1)} collective-permute-done((bf16[640,512]{1,0:T(8,128)(2,1)}, bf16[640,512]{1,0:T(8,128)(2,1)}, u32[]{:S(2)}, u32[]{:S(2)}) %collective-permute-start.17) | collective-permute-done | bytes 655392 | tf_op jit(solution)/shard_map/ppermute | solution.py:23
  86.5 8.7 %all-to-all-start.1 = ((bf16[4,160,512]{2,1,0:T(8,128)(2,1)}), bf16[4,160,512]{2,1,0:T(8,128)(2,1)}, u32[]{:S(2)}, u32[]{:S(2)}) async-start(bf16[4,160,512]{2,1,0:T(8,128)(2,1)} %pad_maximum_fusion.9), calls=%async_computation.1 | async-start | bytes 1310720 | tf_op jit(solution)/shard_map/all_to_all | solution.py:31
  96.3 3.7 %collective-permute-start.20 = (bf16[64,512]{1,0:T(8,128)(2,1)S(1)}, bf16[64,512]{1,0:T(8,128)(2,1)S(1)}, u32[]{:S(2)}, u32[]{:S(2)}) collective-permute-start(bf16[64,512]{1,0:T(8,128)(2,1)S(1)} %get-tuple-element.60), channel_id=1, source_target_pairs={{0,24},{8,0},{16,8},{24,16},{1,25},{9,1},{17,9},{25,17},{2,26},{10... | collective-permute-start | bytes 196616 | tf_op jit(solution)/shard_map/ppermute | solution.py:23
  100.9 2.7 %all-to-all-done.1 = bf16[4,160,512]{2,1,0:T(8,128)(2,1)} async-done(((bf16[4,160,512]{2,1,0:T(8,128)(2,1)}), bf16[4,160,512]{2,1,0:T(8,128)(2,1)}, u32[]{:S(2)}, u32[]{:S(2)}) %all-to-all-start.1) | async-done | bytes 655392 | tf_op jit(solution)/shard_map/all_to_all | solution.py:31
  106.5 2.4 %collective-permute-start.23 = (f32[3,160]{1,0:T(4,128)S(1)}, f32[3,160]{1,0:T(4,128)S(1)}, u32[]{:S(2)}, u32[]{:S(2)}) collective-permute-start(f32[3,160]{1,0:T(4,128)S(1)} %pad_maximum_fusion.15), channel_id=1, source_target_pairs={{0,24},{8,0},{16,8},{24,16},{1,25},{9,1},{17,9},{25,17},{2,26},{10... | collective-permute-start | bytes 5768 | tf_op jit(solution)/shard_map/ppermute | solution.py:23
  110.5 3.3 %collective-permute-done.22 = f32[3,160]{1,0:T(4,128)S(1)} collective-permute-done((f32[3,160]{1,0:T(4,128)S(1)}, f32[3,160]{1,0:T(4,128)S(1)}, u32[]{:S(2)}, u32[]{:S(2)}) %collective-permute-start.22) | collective-permute-done | bytes 1952 | tf_op jit(solution)/shard_map/ppermute | solution.py:23
  114.5 13.7 %all_to_all.20 = bf16[4,160,640]{2,1,0:T(8,128)(2,1)S(1)} all-to-all(bf16[4,160,640]{2,1,0:T(8,128)(2,1)S(1)} %pad_maximum_fusion.4), channel_id=1, replica_groups=mesh['z'=8,'x'=4,'y'=4,'c'=2] {'y'}, dimensions={0} | all-to-all | bytes 1638400 | tf_op jit(solution)/shard_map/all_to_all | solution.py:31
  128.2 3.6 %fusion.41 = (f32[1,160,1024]{2,1,0:T(8,128)}, f32[1,160,1024]{2,1,0:T(8,128)}) fusion(bf16[160,1024]{1,0:T(8,128)(2,1)} %copy-done.5, bf16[160,1024]{1,0:T(8,128)(2,1)S(1)} %copy-done.3, bf16[160,1024]{1,0:T(8,128)(2,1)} %copy-done.6, bf16[160,1024]{1,0:T(8,128)(2,1)} %copy-done.7, bf16[160,1024]{1,0:T(8,128)(2,1)} %copy-done.8, ...), kind=kLoop, calls=%fused_computation.141 | loop fusion | flops 3604480 | bytes 5242880 | tf_op jit(solution)/shard_map/stack | solution.py:111
  134.8 2.2 %fusion.19 = f32[512,1024]{1,0:T(8,128)S(1)} fusion(bf16[640,512]{1,0:T(8,128)(2,1)S(1)} %bitcast.90, bf16[160,1024]{1,0:T(8,128)(2,1)} %collective-permute-done.16, bf16[160,1024]{1,0:T(8,128)(2,1)} %collective-permute-done.15, bf16[160,1024]{1,0:T(8,128)(2,1)S(1)} %copy-done.17, bf16[160,1024]{1,0:T(8,128)(2,1)} %convolution_convert_fusion.3), kind=kOutput, calls=%fused_computation.75 | convolution fusion | flops 676331520 | bytes 4063232 | tf_op jit(solution)/shard_map/dot_general | solution.py:185
  137.0 2.3 %convolution_add_fusion = f32[512,1024]{1,0:T(8,128)S(1)} fusion(f32[512,1024]{1,0:T(8,128)S(1)} %fusion.19, bf16[640,512]{1,0:T(8,128)(2,1)S(1)} %bitcast.80, bf16[160,1024]{1,0:T(8,128)(2,1)} %collective-permute-done.13, bf16[160,1024]{1,0:T(8,128)(2,1)} %collective-permute-done.12, bf16[160,1024]{1,0:T(8,128)(2,1)} %collective-permute-done.11, ...), kind=kOutput, calls=%fused_computation.15 | convolution fusion | flops 676855808 | bytes 6160384 | tf_op jit(solution)/shard_map/dot_general | solution.py:185
  140.2 5.9 %collective-permute-start.31 = (bf16[64,1024]{1,0:T(8,128)(2,1)}, bf16[64,1024]{1,0:T(8,128)(2,1)}, u32[]{:S(2)}, u32[]{:S(2)}) collective-permute-start(bf16[64,1024]{1,0:T(8,128)(2,1)} %get-tuple-element.31), channel_id=1, source_target_pairs={{0,128},{32,160},{64,192},{96,224},{128,0},{160,32},{192,64},{224,... | collective-permute-start | bytes 393224 | tf_op jit(solution)/shard_map/ppermute | solution.py:23
  150.0 8.6 %all-to-all-start.3 = ((bf16[32,2,1280]{2,1,0:T(2,128)(2,1)}), bf16[32,2,1280]{2,1,0:T(2,128)(2,1)}, u32[]{:S(2)}, u32[]{:S(2)}) async-start(bf16[32,2,1280]{2,1,0:T(2,128)(2,1)} %reshape.219), calls=%async_computation.3 | async-start | bytes 327680 | tf_op jit(solution)/shard_map/all_to_all | solution.py:31
  158.6 3.6 %collective-permute-start.29 = (bf16[64,1024]{1,0:T(8,128)(2,1)}, bf16[64,1024]{1,0:T(8,128)(2,1)S(1)}, u32[]{:S(2)}, u32[]{:S(2)}) collective-permute-start(bf16[64,1024]{1,0:T(8,128)(2,1)} %get-tuple-element.33), channel_id=1, source_target_pairs={{0,96},{32,128},{64,160},{96,192},{128,224},{160,0},{192,32},{224,... | collective-permute-start | bytes 393224 | tf_op jit(solution)/shard_map/ppermute | solution.py:23
  165.2 3.0 %collective-permute-start.26 = (bf16[64,1024]{1,0:T(8,128)(2,1)}, bf16[64,1024]{1,0:T(8,128)(2,1)S(1)}, u32[]{:S(2)}, u32[]{:S(2)}) collective-permute-start(bf16[64,1024]{1,0:T(8,128)(2,1)} %get-tuple-element.36), channel_id=1, source_target_pairs={{0,224},{32,0},{64,32},{96,64},{128,96},{160,128},{192,160},{224,1... | collective-permute-start | bytes 393224 | tf_op jit(solution)/shard_map/ppermute | solution.py:23
  168.2 2.5 %pad_maximum_fusion = f32[2,160,1024]{2,1,0:T(8,128)} fusion(f32[1,160,1024]{2,1,0:T(8,128)} %get-tuple-element.54, f32[1,160,1024]{2,1,0:T(8,128)} %get-tuple-element.53), kind=kLoop, calls=%fused_computation.18 | loop fusion | flops 327680 | bytes 2621440 | tf_op jit(solution)/shard_map/stack | solution.py:111
  170.7 5.8 %collective-permute-done.29 = bf16[64,1024]{1,0:T(8,128)(2,1)S(1)} collective-permute-done((bf16[64,1024]{1,0:T(8,128)(2,1)}, bf16[64,1024]{1,0:T(8,128)(2,1)S(1)}, u32[]{:S(2)}, u32[]{:S(2)}) %collective-permute-start.29) | collective-permute-done | bytes 131104 | tf_op jit(solution)/shard_map/ppermute | solution.py:23
  176.5 4.5 %collective-permute-done.27 = bf16[64,1024]{1,0:T(8,128)(2,1)S(1)} collective-permute-done((bf16[64,1024]{1,0:T(8,128)(2,1)}, bf16[64,1024]{1,0:T(8,128)(2,1)S(1)}, u32[]{:S(2)}, u32[]{:S(2)}) %collective-permute-start.27) | collective-permute-done | bytes 131104 | tf_op jit(solution)/shard_map/ppermute | solution.py:23
  (141 shorter events, 46.2 us)
Async XLA Ops:
  6.9 11.1 %collective-permute-start.2 = (bf16[320,1024]{1,0:T(8,128)(2,1)}, bf16[320,1024]{1,0:T(8,128)(2,1)S(1)}, u32[]{:S(2)}, u32[]{:S(2)}) collective-permute-start(bf16[320,1024]{1,0:T(8,128)(2,1)} %get-tuple-element.17), channel_id=1, source_target_pairs={{0,1},{1,0},{2,3},{3,2},{4,5},{5,4},{6,7},{7,6},{8,9},{9,8},{10,11... | collective-permute-start | bytes 1966088 | tf_op jit(solution)/shard_map/ppermute | solution.py:23
  7.0 11.0 %collective-permute-start.3 = (bf16[320,1024]{1,0:T(8,128)(2,1)}, bf16[320,1024]{1,0:T(8,128)(2,1)}, u32[]{:S(2)}, u32[]{:S(2)}) collective-permute-start(bf16[320,1024]{1,0:T(8,128)(2,1)} %get-tuple-element.18), channel_id=1, source_target_pairs={{0,1},{1,0},{2,3},{3,2},{4,5},{5,4},{6,7},{7,6},{8,9},{9,8},{10,11... | collective-permute-start | bytes 1966088 | tf_op jit(solution)/shard_map/ppermute | solution.py:23
  9.1 56.1 %all-to-all-start = ((bf16[8,80,1024]{2,1,0:T(8,128)(2,1)}), bf16[8,80,1024]{2,1,0:T(8,128)(2,1)S(1)}, u32[]{:S(2)}, u32[]{:S(2)}) async-start(bf16[8,80,1024]{2,1,0:T(8,128)(2,1)} %pad_maximum_fusion.2), calls=%async_computation | async-start | bytes 2621440 | tf_op jit(solution)/shard_map/all_to_all | solution.py:31
  17.7 10.2 %collective-permute-start = (bf16[320,1024]{1,0:T(8,128)(2,1)}, bf16[320,1024]{1,0:T(8,128)(2,1)}, u32[]{:S(2)}, u32[]{:S(2)}) collective-permute-start(bf16[320,1024]{1,0:T(8,128)(2,1)} %get-tuple-element.16), channel_id=1, source_target_pairs={{0,1},{1,0},{2,3},{3,2},{4,5},{5,4},{6,7},{7,6},{8,9},{9,8},{10,11... | collective-permute-start | bytes 1966088 | tf_op jit(solution)/shard_map/ppermute | solution.py:23
  25.4 6.5 %collective-permute-start.6 = (bf16[160,1024]{1,0:T(8,128)(2,1)}, bf16[160,1024]{1,0:T(8,128)(2,1)S(1)}, u32[]{:S(2)}, u32[]{:S(2)}) collective-permute-start(bf16[160,1024]{1,0:T(8,128)(2,1)} %get-tuple-element.22), channel_id=1, source_target_pairs={{0,1},{1,0},{2,3},{3,2},{4,5},{5,4},{6,7},{7,6},{8,9},{9,8},{10,11... | collective-permute-start | bytes 983048 | tf_op jit(solution)/shard_map/ppermute | solution.py:23
  25.9 10.8 %collective-permute-start.5 = (bf16[160,1024]{1,0:T(8,128)(2,1)}, bf16[160,1024]{1,0:T(8,128)(2,1)S(1)}, u32[]{:S(2)}, u32[]{:S(2)}) collective-permute-start(bf16[160,1024]{1,0:T(8,128)(2,1)} %get-tuple-element.20), channel_id=1, source_target_pairs={{0,6},{2,0},{4,2},{6,4},{1,7},{3,1},{5,3},{7,5},{8,14},{10,8},{12,... | collective-permute-start | bytes 983048 | tf_op jit(solution)/shard_map/ppermute | solution.py:23
  26.4 19.9 %collective-permute-start.4 = (bf16[160,1024]{1,0:T(8,128)(2,1)}, bf16[160,1024]{1,0:T(8,128)(2,1)S(1)}, u32[]{:S(2)}, u32[]{:S(2)}) collective-permute-start(bf16[160,1024]{1,0:T(8,128)(2,1)} %get-tuple-element.19), channel_id=1, source_target_pairs={{0,2},{2,4},{4,6},{6,0},{1,3},{3,5},{5,7},{7,1},{8,10},{10,12},{12... | collective-permute-start | bytes 983048 | tf_op jit(solution)/shard_map/ppermute | solution.py:23
  30.4 16.8 %collective-permute-start.1 = (bf16[160,1024]{1,0:T(8,128)(2,1)S(1)}, bf16[160,1024]{1,0:T(8,128)(2,1)S(1)}, u32[]{:S(2)}, u32[]{:S(2)}) collective-permute-start(bf16[160,1024]{1,0:T(8,128)(2,1)S(1)} %get-tuple-element.55), channel_id=1, source_target_pairs={{0,4},{2,6},{4,0},{6,2},{1,5},{3,7},{5,1},{7,3},{8,12},{10,14},{12... | collective-permute-start | bytes 983048 | tf_op jit(solution)/shard_map/ppermute | solution.py:23
  31.8 18.1 %collective-permute-start.10 = (bf16[160,1024]{1,0:T(8,128)(2,1)S(1)}, bf16[160,1024]{1,0:T(8,128)(2,1)S(1)}, u32[]{:S(2)}, u32[]{:S(2)}) collective-permute-start(bf16[160,1024]{1,0:T(8,128)(2,1)S(1)} %copy-done.19), channel_id=1, source_target_pairs={{0,1},{1,0},{2,3},{3,2},{4,5},{5,4},{6,7},{7,6},{8,9},{9,8},{10,11... | collective-permute-start | bytes 983048 | tf_op jit(solution)/shard_map/ppermute | solution.py:23
  31.9 20.8 %collective-permute-start.9 = (bf16[160,1024]{1,0:T(8,128)(2,1)S(1)}, bf16[160,1024]{1,0:T(8,128)(2,1)S(1)}, u32[]{:S(2)}, u32[]{:S(2)}) collective-permute-start(bf16[160,1024]{1,0:T(8,128)(2,1)S(1)} %copy-done.18), channel_id=1, source_target_pairs={{0,6},{2,0},{4,2},{6,4},{1,7},{3,1},{5,3},{7,5},{8,14},{10,8},{12,... | collective-permute-start | bytes 983048 | tf_op jit(solution)/shard_map/ppermute | solution.py:23
  36.7 18.2 %collective-permute-start.8 = (bf16[160,1024]{1,0:T(8,128)(2,1)}, bf16[160,1024]{1,0:T(8,128)(2,1)}, u32[]{:S(2)}, u32[]{:S(2)}) collective-permute-start(bf16[160,1024]{1,0:T(8,128)(2,1)} %get-tuple-element.23), channel_id=1, source_target_pairs={{0,2},{2,4},{4,6},{6,0},{1,3},{3,5},{5,7},{7,1},{8,10},{10,12},{12... | collective-permute-start | bytes 983048 | tf_op jit(solution)/shard_map/ppermute | solution.py:23
  46.3 12.3 %collective-permute-start.7 = (bf16[160,1024]{1,0:T(8,128)(2,1)}, bf16[160,1024]{1,0:T(8,128)(2,1)}, u32[]{:S(2)}, u32[]{:S(2)}) collective-permute-start(bf16[160,1024]{1,0:T(8,128)(2,1)} %get-tuple-element.56), channel_id=1, source_target_pairs={{0,4},{2,6},{4,0},{6,2},{1,5},{3,7},{5,1},{7,3},{8,12},{10,14},{12... | collective-permute-start | bytes 983048 | tf_op jit(solution)/shard_map/ppermute | solution.py:23
  48.4 16.9 %collective-permute-start.13 = (bf16[160,1024]{1,0:T(8,128)(2,1)}, bf16[160,1024]{1,0:T(8,128)(2,1)}, u32[]{:S(2)}, u32[]{:S(2)}) collective-permute-start(bf16[160,1024]{1,0:T(8,128)(2,1)} %convolution_convert_fusion.4), channel_id=1, source_target_pairs={{0,8},{8,16},{16,24},{24,0},{1,9},{9,17},{17,25},{25,1},{2,10},{10... | collective-permute-start | bytes 983048 | tf_op jit(solution)/shard_map/ppermute | solution.py:23
  49.9 16.9 %collective-permute-start.12 = (bf16[160,1024]{1,0:T(8,128)(2,1)}, bf16[160,1024]{1,0:T(8,128)(2,1)}, u32[]{:S(2)}, u32[]{:S(2)}) collective-permute-start(bf16[160,1024]{1,0:T(8,128)(2,1)} %convolution_convert_fusion.4), channel_id=1, source_target_pairs={{0,16},{8,24},{16,0},{24,8},{1,17},{9,25},{17,1},{25,9},{2,18},{10... | collective-permute-start | bytes 983048 | tf_op jit(solution)/shard_map/ppermute | solution.py:23
  53.5 16.0 %collective-permute-start.11 = (bf16[160,1024]{1,0:T(8,128)(2,1)}, bf16[160,1024]{1,0:T(8,128)(2,1)}, u32[]{:S(2)}, u32[]{:S(2)}) collective-permute-start(bf16[160,1024]{1,0:T(8,128)(2,1)} %convolution_convert_fusion.4), channel_id=1, source_target_pairs={{0,24},{8,0},{16,8},{24,16},{1,25},{9,1},{17,9},{25,17},{2,26},{10... | collective-permute-start | bytes 983048 | tf_op jit(solution)/shard_map/ppermute | solution.py:23
  61.0 13.1 %collective-permute-start.16 = (bf16[160,1024]{1,0:T(8,128)(2,1)}, bf16[160,1024]{1,0:T(8,128)(2,1)}, u32[]{:S(2)}, u32[]{:S(2)}) collective-permute-start(bf16[160,1024]{1,0:T(8,128)(2,1)} %convolution_convert_fusion.3), channel_id=1, source_target_pairs={{0,8},{8,16},{16,24},{24,0},{1,9},{9,17},{17,25},{25,1},{2,10},{10... | collective-permute-start | bytes 983048 | tf_op jit(solution)/shard_map/ppermute | solution.py:23
  62.5 15.7 %collective-permute-start.15 = (bf16[160,1024]{1,0:T(8,128)(2,1)}, bf16[160,1024]{1,0:T(8,128)(2,1)}, u32[]{:S(2)}, u32[]{:S(2)}) collective-permute-start(bf16[160,1024]{1,0:T(8,128)(2,1)} %convolution_convert_fusion.3), channel_id=1, source_target_pairs={{0,16},{8,24},{16,0},{24,8},{1,17},{9,25},{17,1},{25,9},{2,18},{10... | collective-permute-start | bytes 983048 | tf_op jit(solution)/shard_map/ppermute | solution.py:23
  65.4 12.9 %collective-permute-start.14 = (bf16[160,1024]{1,0:T(8,128)(2,1)}, bf16[160,1024]{1,0:T(8,128)(2,1)S(1)}, u32[]{:S(2)}, u32[]{:S(2)}) collective-permute-start(bf16[160,1024]{1,0:T(8,128)(2,1)} %convolution_convert_fusion.3), channel_id=1, source_target_pairs={{0,24},{8,0},{16,8},{24,16},{1,25},{9,1},{17,9},{25,17},{2,26},{10... | collective-permute-start | bytes 983048 | tf_op jit(solution)/shard_map/ppermute | solution.py:23
  86.5 17.1 %all-to-all-start.1 = ((bf16[4,160,512]{2,1,0:T(8,128)(2,1)}), bf16[4,160,512]{2,1,0:T(8,128)(2,1)}, u32[]{:S(2)}, u32[]{:S(2)}) async-start(bf16[4,160,512]{2,1,0:T(8,128)(2,1)} %pad_maximum_fusion.9), calls=%async_computation.1 | async-start | bytes 1310720 | tf_op jit(solution)/shard_map/all_to_all | solution.py:31
  96.3 8.5 %collective-permute-start.20 = (bf16[64,512]{1,0:T(8,128)(2,1)S(1)}, bf16[64,512]{1,0:T(8,128)(2,1)S(1)}, u32[]{:S(2)}, u32[]{:S(2)}) collective-permute-start(bf16[64,512]{1,0:T(8,128)(2,1)S(1)} %get-tuple-element.60), channel_id=1, source_target_pairs={{0,24},{8,0},{16,8},{24,16},{1,25},{9,1},{17,9},{25,17},{2,26},{10... | collective-permute-start | bytes 196616 | tf_op jit(solution)/shard_map/ppermute | solution.py:23
  99.9 5.8 %collective-permute-start.19 = (bf16[64,512]{1,0:T(8,128)(2,1)S(1)}, bf16[64,512]{1,0:T(8,128)(2,1)S(1)}, u32[]{:S(2)}, u32[]{:S(2)}) collective-permute-start(bf16[64,512]{1,0:T(8,128)(2,1)S(1)} %get-tuple-element.61), channel_id=1, source_target_pairs={{0,16},{8,24},{16,0},{24,8},{1,17},{9,25},{17,1},{25,9},{2,18},{10... | collective-permute-start | bytes 196616 | tf_op jit(solution)/shard_map/ppermute | solution.py:23
  99.9 6.2 %collective-permute-start.18 = (bf16[64,512]{1,0:T(8,128)(2,1)S(1)}, bf16[64,512]{1,0:T(8,128)(2,1)S(1)}, u32[]{:S(2)}, u32[]{:S(2)}) collective-permute-start(bf16[64,512]{1,0:T(8,128)(2,1)S(1)} %get-tuple-element.62), channel_id=1, source_target_pairs={{0,8},{8,16},{16,24},{24,0},{1,9},{9,17},{17,25},{25,1},{2,10},{10... | collective-permute-start | bytes 196616 | tf_op jit(solution)/shard_map/ppermute | solution.py:23
  108.9 4.8 %collective-permute-start.22 = (f32[3,160]{1,0:T(4,128)S(1)}, f32[3,160]{1,0:T(4,128)S(1)}, u32[]{:S(2)}, u32[]{:S(2)}) collective-permute-start(f32[3,160]{1,0:T(4,128)S(1)} %pad_maximum_fusion.15), channel_id=1, source_target_pairs={{0,8},{8,16},{16,24},{24,0},{1,9},{9,17},{17,25},{25,1},{2,10},{10... | collective-permute-start | bytes 5768 | tf_op jit(solution)/shard_map/ppermute | solution.py:23
  108.9 5.1 %collective-permute-start.21 = (f32[3,160]{1,0:T(4,128)S(1)}, f32[3,160]{1,0:T(4,128)S(1)}, u32[]{:S(2)}, u32[]{:S(2)}) collective-permute-start(f32[3,160]{1,0:T(4,128)S(1)} %pad_maximum_fusion.15), channel_id=1, source_target_pairs={{0,16},{8,24},{16,0},{24,8},{1,17},{9,25},{17,1},{25,9},{2,18},{10... | collective-permute-start | bytes 5768 | tf_op jit(solution)/shard_map/ppermute | solution.py:23
  140.2 25.0 %collective-permute-start.31 = (bf16[64,1024]{1,0:T(8,128)(2,1)}, bf16[64,1024]{1,0:T(8,128)(2,1)}, u32[]{:S(2)}, u32[]{:S(2)}) collective-permute-start(bf16[64,1024]{1,0:T(8,128)(2,1)} %get-tuple-element.31), channel_id=1, source_target_pairs={{0,128},{32,160},{64,192},{96,224},{128,0},{160,32},{192,64},{224,... | collective-permute-start | bytes 393224 | tf_op jit(solution)/shard_map/ppermute | solution.py:23
  146.1 22.0 %collective-permute-start.30 = (bf16[64,1024]{1,0:T(8,128)(2,1)}, bf16[64,1024]{1,0:T(8,128)(2,1)}, u32[]{:S(2)}, u32[]{:S(2)}) collective-permute-start(bf16[64,1024]{1,0:T(8,128)(2,1)} %get-tuple-element.32), channel_id=1, source_target_pairs={{0,160},{32,192},{64,224},{96,0},{128,32},{160,64},{192,96},{224,1... | collective-permute-start | bytes 393224 | tf_op jit(solution)/shard_map/ppermute | solution.py:23
  150.0 34.4 %all-to-all-start.3 = ((bf16[32,2,1280]{2,1,0:T(2,128)(2,1)}), bf16[32,2,1280]{2,1,0:T(2,128)(2,1)}, u32[]{:S(2)}, u32[]{:S(2)}) async-start(bf16[32,2,1280]{2,1,0:T(2,128)(2,1)} %reshape.219), calls=%async_computation.3 | async-start | bytes 327680 | tf_op jit(solution)/shard_map/all_to_all | solution.py:31
  158.6 17.8 %collective-permute-start.29 = (bf16[64,1024]{1,0:T(8,128)(2,1)}, bf16[64,1024]{1,0:T(8,128)(2,1)S(1)}, u32[]{:S(2)}, u32[]{:S(2)}) collective-permute-start(bf16[64,1024]{1,0:T(8,128)(2,1)} %get-tuple-element.33), channel_id=1, source_target_pairs={{0,96},{32,128},{64,160},{96,192},{128,224},{160,0},{192,32},{224,... | collective-permute-start | bytes 393224 | tf_op jit(solution)/shard_map/ppermute | solution.py:23
  162.2 14.2 %collective-permute-start.28 = (bf16[64,1024]{1,0:T(8,128)(2,1)}, bf16[64,1024]{1,0:T(8,128)(2,1)S(1)}, u32[]{:S(2)}, u32[]{:S(2)}) collective-permute-start(bf16[64,1024]{1,0:T(8,128)(2,1)} %get-tuple-element.34), channel_id=1, source_target_pairs={{0,192},{32,224},{64,0},{96,32},{128,64},{160,96},{192,128},{224,1... | collective-permute-start | bytes 393224 | tf_op jit(solution)/shard_map/ppermute | solution.py:23
  164.0 17.0 %collective-permute-start.27 = (bf16[64,1024]{1,0:T(8,128)(2,1)}, bf16[64,1024]{1,0:T(8,128)(2,1)S(1)}, u32[]{:S(2)}, u32[]{:S(2)}) collective-permute-start(bf16[64,1024]{1,0:T(8,128)(2,1)} %get-tuple-element.35), channel_id=1, source_target_pairs={{0,64},{32,96},{64,128},{96,160},{128,192},{160,224},{192,0},{224,... | collective-permute-start | bytes 393224 | tf_op jit(solution)/shard_map/ppermute | solution.py:23
  165.2 15.8 %collective-permute-start.26 = (bf16[64,1024]{1,0:T(8,128)(2,1)}, bf16[64,1024]{1,0:T(8,128)(2,1)S(1)}, u32[]{:S(2)}, u32[]{:S(2)}) collective-permute-start(bf16[64,1024]{1,0:T(8,128)(2,1)} %get-tuple-element.36), channel_id=1, source_target_pairs={{0,224},{32,0},{64,32},{96,64},{128,96},{160,128},{192,160},{224,1... | collective-permute-start | bytes 393224 | tf_op jit(solution)/shard_map/ppermute | solution.py:23
  168.2 14.4 %collective-permute-start.25 = (bf16[64,1024]{1,0:T(8,128)(2,1)S(1)}, bf16[64,1024]{1,0:T(8,128)(2,1)S(1)}, u32[]{:S(2)}, u32[]{:S(2)}) collective-permute-start(bf16[64,1024]{1,0:T(8,128)(2,1)S(1)} %get-tuple-element.30), channel_id=1, source_target_pairs={{0,32},{32,64},{64,96},{96,128},{128,160},{160,192},{192,224},{224... | collective-permute-start | bytes 393224 | tf_op jit(solution)/shard_map/ppermute | solution.py:23
  (23 other events, 151.5 us)
